TPU v7x, 32 devices: a whole 2x2x4 slice. The times are simulated.
32 devices in a mesh: groups: 2 (over x), rows: 16 (over z, y, core).
Axes of the slice: x: 2, y: 2, z: 4, core: 2. Of those that a mesh axis runs over, the one named last changes fastest.
Arguments:
- features: bfloat16 [32768, 384], P(('groups', 'rows')), parts along dimension 0, may hold values from -8 to 8
- iterate: float32 [32768, 64], P(('groups', 'rows')), parts along dimension 0, may hold values from -6 to 6
- band_mask: int32 [32, 2], P(('groups', 'rows')), parts along dimension 0, may hold values from 0 to 1, as said below
Outputs:
- eigvecs: float32 [32768, 64], P(('groups', 'rows')), parts along dimension 0
- degrees: float32 [32768], P(('groups', 'rows')), parts along dimension 0
There are 2 independent parts, one for each index of `groups`. A program takes and returns all parts, laid end to end along the dimension named above; each array names one. Nothing has to cross between parts.
Inputs may be any that keep to these rules, and one draw needn't show every extreme that they name: band_mask[i, o] is 0 wherever i + o + 1 >= 16, and 1 wherever i + o + 1 == 15.
All inputs are finite; a program needn't handle non-finite values.
Results may differ from a plain program's by a relative error of at most 0.0067.
Values may be sent and summed in bfloat16 or wider, within the bound.
A program may use at most 64 MiB of HBM per device.

v0:
```python
import jax
import jax.numpy as jnp
from jax import lax
from jax.sharding import PartitionSpec as P

W = 2
ITERS = 2


def shifted(array, axis, by):
    peers = lax.axis_size(axis)
    pairs = [(i, i + by) for i in range(peers) if 0 <= i + by < peers]
    return lax.ppermute(array, axis, pairs)


def unit_rows(features):
    values = features.astype(jnp.float32)
    return (values * lax.rsqrt(jnp.sum(values * values, axis=-1, keepdims=True) + 1e-06)).astype(
        jnp.bfloat16
    )


def affinity(left, right):
    count = left.shape[0]
    step = min(512, count)
    pieces = []
    for start in range(0, count, step):
        scores = lax.dot_general(
            left[start : start + step],
            right,
            (((1,), (1,)), ((), ())),
            preferred_element_type=jnp.float32,
        )
        pieces.append(jnp.exp(scores).astype(jnp.bfloat16))
    return jnp.concatenate(pieces, 0)


def local(features, iterate, band_mask):
    unit = unit_rows(features)
    keep_row = band_mask[0]
    reach = W
    partners = []
    for offset in range(1, reach + 1):
        partners.append(shifted(unit, "rows", -offset))
    tiles = [affinity(unit, unit)]
    for offset in range(1, reach + 1):
        keep = keep_row[offset - 1]
        partner = partners[offset - 1]
        tiles.append(affinity(unit, partner) * keep.astype(jnp.bfloat16))
    degrees = jnp.sum(tiles[0].astype(jnp.float32), axis=1)
    for offset in range(1, reach + 1):
        degrees = degrees + jnp.sum(tiles[offset].astype(jnp.float32), axis=1)
    for offset in range(1, reach + 1):
        column_sums = jnp.sum(tiles[offset].astype(jnp.float32), axis=0)
        degrees = degrees + shifted(column_sums, "rows", offset)
    scale = lax.rsqrt(degrees)[:, None]
    current = iterate
    for step in range(ITERS):
        scaled = (current * scale).astype(jnp.bfloat16)
        neighbours = []
        for offset in range(1, reach + 1):
            neighbours.append(shifted(scaled, "rows", -offset))
        image = jnp.dot(tiles[0], scaled, preferred_element_type=jnp.float32)
        for offset in range(1, reach + 1):
            image = image + jnp.dot(
                tiles[offset], neighbours[offset - 1], preferred_element_type=jnp.float32
            )
        for offset in range(1, reach + 1):
            mirrored = lax.dot_general(
                tiles[offset], scaled, (((0,), (0,)), ((), ())), preferred_element_type=jnp.float32
            )
            image = image + shifted(mirrored, "rows", offset)
        normed = image * scale
        local_gram = lax.dot_general(
            normed,
            normed,
            (((0,), (0,)), ((), ())),
            precision=lax.Precision.HIGHEST,
            preferred_element_type=jnp.float32,
        )
        gram = lax.psum(local_gram, "rows")
        lower = jnp.linalg.cholesky(gram)
        current = jax.scipy.linalg.solve_triangular(lower, normed.T, lower=True).T
    return (current, degrees)


def solution(mesh):
    return jax.shard_map(
        local,
        mesh=mesh,
        in_specs=(
            P(("groups", "rows"), None),
            P(("groups", "rows"), None),
            P(("groups", "rows"), None),
        ),
        out_specs=(P(("groups", "rows"), None), P(("groups", "rows"))),
        check_vma=False,
    )
```

profile of v0, /device:TPU:0, one launch (start us, length us, event | category | flops | bytes accessed | tf_op | source)
XLA Modules:
  0.0 225.3 jit_solution(5251007546678037739)
XLA Ops:
  0.6 1.4 fusion
  2.1 0.2 fusion.1
  2.3 1.3 collective-permute-start.1
  3.6 1.3 collective-permute-start
  4.9 0.7 exponential_convert_fusion.4
  5.7 0.7 exponential_convert_fusion.5
  6.5 0.6 fusion.34
  7.1 17.7 %collective-permute-done.1 = bf16[1024,384]{1,0:T(8,128)(2,1)S(1)} collective-permute-done((bf16[1024,384]{1,0:T(8,128)(2,1)S(1)}, bf16[1024,384]{1,0:T(8,128)(2,1)S(1)}, u32[]{:S(2)}, u32[]{:S(2)}) %collective-permute-start.1) | collective-permute-done | bytes 786464 | tf_op jit(solution)/shard_map/ppermute | solution.py:13
  24.8 0.7 exponential_convert_fusion
  25.5 0.7 exponential_convert_fusion.1
  26.3 1.2 convert_reduce_fusion.1
  27.4 4.5 %collective-permute-start.3 = (f32[1024]{0:T(1024)S(1)}, f32[1024]{0:T(1024)S(1)}, u32[]{:S(2)}, u32[]{:S(2)}) collective-permute-start(f32[1024]{0:T(1024)S(1)} %get-tuple-element.7), channel_id=1, source_target_pairs={{0,2},{1,3},{2,4},{3,5},{4,6},{5,7},{6,8},{7,9},{8,10},{9,11},{10,... | collective-permute-start | bytes 12296 | tf_op jit(solution)/shard_map/ppermute | solution.py:13
  32.0 0.0 collective-permute-done
  32.0 0.7 exponential_convert_fusion.2
  32.7 0.7 exponential_convert_fusion.3
  33.5 1.3 convert_reduce_fusion.3
  34.8 0.0 copy-start.7
  34.8 3.1 %collective-permute-start.2 = (f32[1024]{0:T(1024)S(1)}, f32[1024]{0:T(1024)S(1)}, u32[]{:S(2)}, u32[]{:S(2)}) collective-permute-start(f32[1024]{0:T(1024)S(1)} %get-tuple-element.5), channel_id=1, source_target_pairs={{0,1},{1,2},{2,3},{3,4},{4,5},{5,6},{6,7},{7,8},{8,9},{9,10},{10,1... | collective-permute-start | bytes 12296 | tf_op jit(solution)/shard_map/ppermute | solution.py:13
  37.9 0.3 convert_reduce_fusion.4
  38.2 0.0 collective-permute-done.3
  38.2 0.4 collective-permute-done.2
  38.7 0.6 fusion.33
  39.3 1.1 fusion.29
  40.4 1.2 fusion.31
  41.6 1.3 collective-permute-start.4
  42.9 5.3 %collective-permute-start.7 = (f32[1024,64]{0,1:T(8,128)S(1)}, f32[1024,64]{0,1:T(8,128)S(1)}, u32[]{:S(2)}, u32[]{:S(2)}) collective-permute-start(f32[1024,64]{0,1:T(8,128)S(1)} %fusion.29), channel_id=1, source_target_pairs={{0,2},{1,3},{2,4},{3,5},{4,6},{5,7},{6,8},{7,9},{8,10},{9,11},{10,... | collective-permute-start | bytes 786440 | tf_op jit(solution)/shard_map/ppermute | solution.py:13
  48.1 2.1 collective-permute-start.6
  50.3 0.8 fusion.10
  51.1 1.3 collective-permute-start.5
  52.4 0.0 collective-permute-done.4
  52.4 1.4 convolution_add_fusion.3
  53.8 5.6 %collective-permute-done.5 = bf16[1024,64]{0,1:T(8,128)(2,1)S(1)} collective-permute-done((bf16[1024,64]{0,1:T(8,128)(2,1)S(1)}, bf16[1024,64]{0,1:T(8,128)(2,1)S(1)}, u32[]{:S(2)}, u32[]{:S(2)}) %collective-permute-start.5) | collective-permute-done | bytes 131104 | tf_op jit(solution)/shard_map/ppermute | solution.py:13
  59.4 0.0 collective-permute-done.7
  59.4 0.0 collective-permute-done.6
  59.4 1.3 fusion.6
  60.7 0.4 fusion.35
  61.0 63.7 %psum.14 = f32[64,64]{0,1:T(8,128)S(1)} all-reduce(f32[64,64]{0,1:T(8,128)S(1)} %fusion.35), channel_id=1, replica_groups=mesh['groups'=2,'rows'=16] {'rows'}, use_global_device_ids=true, to_apply=%region_6.0 | all-reduce | flops 4096 | bytes 32768 | tf_op jit(solution)/shard_map/psum | solution.py:81
  124.7 0.1 copy.6
  124.8 5.8 %cholesky.44 = f32[64,64]{1,0:T(8,128)S(1)} custom-call(f32[64,64]{1,0:T(8,128)S(1)} %fusion.24), custom_call_target="Cholesky" | custom-call | tf_op jit(solution)/shard_map/jit(cholesky)/cholesky | solution.py:82
  130.7 0.7 compare_reduce_fusion.1
  131.4 0.6 fusion.19
  132.0 4.9 %custom-call.6 = f32[1,64,64]{1,2,0:T(8,128)S(1)} custom-call(f32[1,64,64]{2,1,0:T(8,128)S(1)} %fusion.19), custom_call_target="InvertDiagBlocksLowerTriangular" | custom-call | tf_op jit(solution)/shard_map/jit(_solve_triangular)/triangular_solve | solution.py:83
  136.9 0.4 fusion.8
  137.3 1.2 fusion.30
  138.5 0.1 copy-done.2
  138.6 1.3 fusion.32
  139.9 1.3 collective-permute-start.11
  141.2 1.3 collective-permute-start.10
  142.5 1.3 collective-permute-start.8
  143.8 0.8 fusion.9
  144.6 1.3 collective-permute-start.9
  145.9 1.4 convolution_add_fusion.1
  147.3 5.4 %collective-permute-done.9 = bf16[1024,64]{0,1:T(8,128)(2,1)S(1)} collective-permute-done((bf16[1024,64]{0,1:T(8,128)(2,1)S(1)}, bf16[1024,64]{0,1:T(8,128)(2,1)S(1)}, u32[]{:S(2)}, u32[]{:S(2)}) %collective-permute-start.9) | collective-permute-done | bytes 131104 | tf_op jit(solution)/shard_map/ppermute | solution.py:13
  152.7 0.0 collective-permute-done.11
  152.7 0.0 collective-permute-done.10
  152.7 1.3 fusion.7
  154.0 0.4 fusion.36
  154.4 57.6 %psum.15 = f32[64,64]{0,1:T(8,128)S(1)} all-reduce(f32[64,64]{0,1:T(8,128)S(1)} %fusion.36), channel_id=1, replica_groups=mesh['groups'=2,'rows'=16] {'rows'}, use_global_device_ids=true, to_apply=%region_9.12 | all-reduce | flops 4096 | bytes 32768 | tf_op jit(solution)/shard_map/psum | solution.py:81
  212.0 0.1 copy.8
  212.1 5.8 %cholesky.55 = f32[64,64]{1,0:T(8,128)S(1)} custom-call(f32[64,64]{1,0:T(8,128)S(1)} %fusion.22), custom_call_target="Cholesky" | custom-call | tf_op jit(solution)/shard_map/jit(cholesky)/cholesky | solution.py:82
  218.0 0.6 compare_reduce_fusion
  218.6 0.7 fusion.20
  219.3 4.9 %custom-call.7 = f32[1,64,64]{1,2,0:T(8,128)S(1)} custom-call(f32[1,64,64]{2,1,0:T(8,128)S(1)} %fusion.20), custom_call_target="InvertDiagBlocksLowerTriangular" | custom-call | tf_op jit(solution)/shard_map/jit(_solve_triangular)/triangular_solve | solution.py:83
  224.2 1.1 convolution_bitcast_fusion
  (24 shorter events, 0.1 us)
Async XLA Ops:
  0.6 1.5 copy-start
  0.6 4.3 %copy-start.8 = (s32[1,2]{1,0:T(1,128)S(1)}, s32[1,2]{1,0:T(1,128)}, u32[]{:S(2)}) copy-start(s32[1,2]{1,0:T(1,128)} %param.8) | copy-start | bytes 28
  2.3 22.4 %collective-permute-start.1 = (bf16[1024,384]{1,0:T(8,128)(2,1)S(1)}, bf16[1024,384]{1,0:T(8,128)(2,1)S(1)}, u32[]{:S(2)}, u32[]{:S(2)}) collective-permute-start(bf16[1024,384]{1,0:T(8,128)(2,1)S(1)} %fusion.1), channel_id=1, source_target_pairs={{2,0},{3,1},{4,2},{5,3},{6,4},{7,5},{8,6},{9,7},{10,8},{11,9},{12,... | collective-permute-start | bytes 2359304 | tf_op jit(solution)/shard_map/ppermute | solution.py:13
  3.6 28.4 %collective-permute-start = (bf16[1024,384]{1,0:T(8,128)(2,1)S(1)}, bf16[1024,384]{1,0:T(8,128)(2,1)S(1)}, u32[]{:S(2)}, u32[]{:S(2)}) collective-permute-start(bf16[1024,384]{1,0:T(8,128)(2,1)S(1)} %fusion.1), channel_id=1, source_target_pairs={{1,0},{2,1},{3,2},{4,3},{5,4},{6,5},{7,6},{8,7},{9,8},{10,9},{11,1... | collective-permute-start | bytes 2359304 | tf_op jit(solution)/shard_map/ppermute | solution.py:13
  5.7 44.6 %copy-start.3 = (bf16[512,1024]{1,0:T(8,128)(2,1)}, bf16[512,1024]{1,0:T(8,128)(2,1)S(1)}, u32[]{:S(2)}) copy-start(bf16[512,1024]{1,0:T(8,128)(2,1)S(1)} %exponential_convert_fusion.4) | copy-start | bytes 3145732
  6.5 43.8 %copy-start.5 = (bf16[512,1024]{1,0:T(8,128)(2,1)}, bf16[512,1024]{1,0:T(8,128)(2,1)S(1)}, u32[]{:S(2)}) copy-start(bf16[512,1024]{1,0:T(8,128)(2,1)S(1)} %exponential_convert_fusion.5) | copy-start | bytes 3145732
  27.4 10.8 %collective-permute-start.3 = (f32[1024]{0:T(1024)S(1)}, f32[1024]{0:T(1024)S(1)}, u32[]{:S(2)}, u32[]{:S(2)}) collective-permute-start(f32[1024]{0:T(1024)S(1)} %get-tuple-element.7), channel_id=1, source_target_pairs={{0,2},{1,3},{2,4},{3,5},{4,6},{5,7},{6,8},{7,9},{8,10},{9,11},{10,... | collective-permute-start | bytes 12296 | tf_op jit(solution)/shard_map/ppermute | solution.py:13
  33.5 18.9 %copy-start.1 = (bf16[512,1024]{1,0:T(8,128)(2,1)}, bf16[512,1024]{1,0:T(8,128)(2,1)S(1)}, u32[]{:S(2)}) copy-start(bf16[512,1024]{1,0:T(8,128)(2,1)S(1)} %exponential_convert_fusion.3) | copy-start | bytes 3145732
  34.8 4.5 %copy-start.7 = (f32[1024,64]{0,1:T(8,128)S(1)}, f32[1024,64]{0,1:T(8,128)}, u32[]{:S(2)}) copy-start(f32[1024,64]{0,1:T(8,128)} %param.7) | copy-start | bytes 786436
  34.8 3.9 %collective-permute-start.2 = (f32[1024]{0:T(1024)S(1)}, f32[1024]{0:T(1024)S(1)}, u32[]{:S(2)}, u32[]{:S(2)}) collective-permute-start(f32[1024]{0:T(1024)S(1)} %get-tuple-element.5), channel_id=1, source_target_pairs={{0,1},{1,2},{2,3},{3,4},{4,5},{5,6},{6,7},{7,8},{8,9},{9,10},{10,1... | collective-permute-start | bytes 12296 | tf_op jit(solution)/shard_map/ppermute | solution.py:13
  41.6 10.8 %collective-permute-start.4 = (bf16[1024,64]{0,1:T(8,128)(2,1)S(1)}, bf16[1024,64]{0,1:T(8,128)(2,1)S(1)}, u32[]{:S(2)}, u32[]{:S(2)}) collective-permute-start(bf16[1024,64]{0,1:T(8,128)(2,1)S(1)} %multiply_convert_fusion), channel_id=1, source_target_pairs={{1,0},{2,1},{3,2},{4,3},{5,4},{6,5},{7,6},{8,7},{9,8},{10,9},{11,1... | collective-permute-start | bytes 393224 | tf_op jit(solution)/shard_map/ppermute | solution.py:13
  42.9 16.5 %collective-permute-start.7 = (f32[1024,64]{0,1:T(8,128)S(1)}, f32[1024,64]{0,1:T(8,128)S(1)}, u32[]{:S(2)}, u32[]{:S(2)}) collective-permute-start(f32[1024,64]{0,1:T(8,128)S(1)} %fusion.29), channel_id=1, source_target_pairs={{0,2},{1,3},{2,4},{3,5},{4,6},{5,7},{6,8},{7,9},{8,10},{9,11},{10,... | collective-permute-start | bytes 786440 | tf_op jit(solution)/shard_map/ppermute | solution.py:13
  48.1 11.2 %collective-permute-start.6 = (f32[1024,64]{0,1:T(8,128)S(1)}, f32[1024,64]{0,1:T(8,128)S(1)}, u32[]{:S(2)}, u32[]{:S(2)}) collective-permute-start(f32[1024,64]{0,1:T(8,128)S(1)} %fusion.31), channel_id=1, source_target_pairs={{0,1},{1,2},{2,3},{3,4},{4,5},{5,6},{6,7},{7,8},{8,9},{9,10},{10,1... | collective-permute-start | bytes 786440 | tf_op jit(solution)/shard_map/ppermute | solution.py:13
  51.1 8.3 %collective-permute-start.5 = (bf16[1024,64]{0,1:T(8,128)(2,1)S(1)}, bf16[1024,64]{0,1:T(8,128)(2,1)S(1)}, u32[]{:S(2)}, u32[]{:S(2)}) collective-permute-start(bf16[1024,64]{0,1:T(8,128)(2,1)S(1)} %multiply_convert_fusion), channel_id=1, source_target_pairs={{2,0},{3,1},{4,2},{5,3},{6,4},{7,5},{8,6},{9,7},{10,8},{11,9},{12,... | collective-permute-start | bytes 393224 | tf_op jit(solution)/shard_map/ppermute | solution.py:13
  137.3 1.2 copy-start.2
  138.5 5.3 %copy-start.4 = (bf16[512,1024]{1,0:T(8,128)(2,1)S(1)}, bf16[512,1024]{1,0:T(8,128)(2,1)}, u32[]{:S(2)}) copy-start(bf16[512,1024]{1,0:T(8,128)(2,1)} %copy-done.3) | copy-start | bytes 3145732
  138.6 5.3 %copy-start.6 = (bf16[512,1024]{1,0:T(8,128)(2,1)S(1)}, bf16[512,1024]{1,0:T(8,128)(2,1)}, u32[]{:S(2)}) copy-start(bf16[512,1024]{1,0:T(8,128)(2,1)} %copy-done.5) | copy-start | bytes 3145732
  139.9 12.8 %collective-permute-start.11 = (f32[1024,64]{0,1:T(8,128)S(1)}, f32[1024,64]{0,1:T(8,128)S(1)}, u32[]{:S(2)}, u32[]{:S(2)}) collective-permute-start(f32[1024,64]{0,1:T(8,128)S(1)} %fusion.30), channel_id=1, source_target_pairs={{0,2},{1,3},{2,4},{3,5},{4,6},{5,7},{6,8},{7,9},{8,10},{9,11},{10,... | collective-permute-start | bytes 786440 | tf_op jit(solution)/shard_map/ppermute | solution.py:13
  141.2 11.5 %collective-permute-start.10 = (f32[1024,64]{0,1:T(8,128)S(1)}, f32[1024,64]{0,1:T(8,128)S(1)}, u32[]{:S(2)}, u32[]{:S(2)}) collective-permute-start(f32[1024,64]{0,1:T(8,128)S(1)} %fusion.32), channel_id=1, source_target_pairs={{0,1},{1,2},{2,3},{3,4},{4,5},{5,6},{6,7},{7,8},{8,9},{9,10},{10,1... | collective-permute-start | bytes 786440 | tf_op jit(solution)/shard_map/ppermute | solution.py:13
  142.5 3.4 %collective-permute-start.8 = (bf16[1024,64]{0,1:T(8,128)(2,1)S(1)}, bf16[1024,64]{0,1:T(8,128)(2,1)S(1)}, u32[]{:S(2)}, u32[]{:S(2)}) collective-permute-start(bf16[1024,64]{0,1:T(8,128)(2,1)S(1)} %bitcast.49), channel_id=1, source_target_pairs={{1,0},{2,1},{3,2},{4,3},{5,4},{6,5},{7,6},{8,7},{9,8},{10,9},{11,1... | collective-permute-start | bytes 393224 | tf_op jit(solution)/shard_map/ppermute | solution.py:13
  144.6 8.1 %collective-permute-start.9 = (bf16[1024,64]{0,1:T(8,128)(2,1)S(1)}, bf16[1024,64]{0,1:T(8,128)(2,1)S(1)}, u32[]{:S(2)}, u32[]{:S(2)}) collective-permute-start(bf16[1024,64]{0,1:T(8,128)(2,1)S(1)} %bitcast.50), channel_id=1, source_target_pairs={{2,0},{3,1},{4,2},{5,3},{6,4},{7,5},{8,6},{9,7},{10,8},{11,9},{12,... | collective-permute-start | bytes 393224 | tf_op jit(solution)/shard_map/ppermute | solution.py:13
where the time goes:
time: 226 us; the launch traced here: 225 us
  blocking collectives  121 us (54%)
  other arithmetic  29.2 us (13%)
  waiting for transfers between devices  29.1 us (13%)
  starting transfers between devices  25.4 us (11%)
  matrix products  18.5 us (8%)
    psum x2, blocking collectives, local(): gram = lax.psum(local_gram, 'rows')  121 us
    ppermute x12, waiting for transfers between devices, shifted(): return lax.ppermute(array, axis, pairs)  29.1 us
    ppermute x12, starting transfers between devices, shifted(): return lax.ppermute(array, axis, pairs)  25.4 us
    another operation x6, other arithmetic, local(): lower = jnp.linalg.cholesky(gram)  13.1 us
    another operation x4, other arithmetic, local(): current = jax.scipy.linalg.solve_triangular(lower, normed.T, lower=True).T  11.1 us
    dot_general x4, matrix products, local(): jnp.dot(tiles[offset], neighbours[offset - 1], preferred_element_type=jnp...  5.45 us
    dot_general x4, matrix products, local(): lax.dot_general(tiles[offset], scaled, (((0,), (0,)), ((), ())), preferre...  4.76 us
  transfers between devices with their start and end apart: 12, of which 4 were waited for; matrix products, arithmetic and copies ran while one was open for 5% of the time, Pallas kernels for 0%

commit v1 on v0

--- a/solution.py
+++ b/solution.py
@@ -1,10 +1,150 @@
+import functools
+
 import jax
 import jax.numpy as jnp
 from jax import lax
+from jax.experimental import pallas as pl
+from jax.experimental.pallas import tpu as pltpu
 from jax.sharding import PartitionSpec as P
 
 W = 2
 ITERS = 2
+AXIS = "rows"
+MESH = pl.DeviceIdType.MESH
+HIGH = lax.Precision.HIGHEST
+
+
+def radices(count):
+    out = []
+    while count > 1:
+        radix = next((r for r in (4, 2, 3, 5, 7) if count % r == 0), count)
+        out.append(radix)
+        count //= radix
+    return out
+
+
+def peers_of(me, plan):
+    stride = 1
+    found = []
+    for radix in plan:
+        digit = lax.rem(lax.div(me, stride), radix)
+        row = []
+        for k in range(1, radix):
+            other = lax.rem(digit + k, radix)
+            row.append((other, me + (other - digit) * stride))
+        found.append((digit, row))
+        stride *= radix
+    return found
+
+
+def all_sum(value, found, box, send_sem, recv_sem):
+    for phase, (digit, row) in enumerate(found):
+        box[phase, digit] = value
+        copies = []
+        for k, (other, peer) in enumerate(row):
+            copy = pltpu.make_async_remote_copy(
+                src_ref=box.at[phase, digit],
+                dst_ref=box.at[phase, digit],
+                send_sem=send_sem.at[phase, k],
+                recv_sem=recv_sem.at[phase, digit],
+                device_id={AXIS: peer},
+                device_id_type=MESH,
+            )
+            copy.start()
+            copies.append(copy)
+        for other, peer in row:
+            pltpu.make_async_remote_copy(
+                src_ref=box.at[phase, other],
+                dst_ref=box.at[phase, other],
+                send_sem=send_sem.at[phase, 0],
+                recv_sem=recv_sem.at[phase, other],
+                device_id={AXIS: peer},
+                device_id_type=MESH,
+            ).wait_recv()
+        value = box[phase, 0]
+        for slot in range(1, len(row) + 1):
+            value = value + box[phase, slot]
+        for copy in copies:
+            copy.wait_send()
+    return value
+
+
+def inverse_factor(gram):
+    size = gram.shape[0]
+    rows = lax.broadcasted_iota(jnp.int32, (size, size), 0)
+    cols = lax.broadcasted_iota(jnp.int32, (size, size), 1)
+    both = jnp.concatenate([gram, jnp.where(rows == cols, 1.0, 0.0)], axis=1)
+    count = size // 8
+    bands = [both[8 * b : 8 * b + 8] for b in range(count)]
+    sub = lax.broadcasted_iota(jnp.int32, (8, 1), 0)
+    pivots = []
+    for j in range(size):
+        b, s = j // 8, j % 8
+        row = bands[b][s : s + 1]
+        pivot = row[:, j : j + 1]
+        pivots.append(pivot)
+        scaled = row * (1.0 / pivot)
+        for c in range(b, count):
+            column = bands[c][:, j : j + 1]
+            if c == b:
+                column = jnp.where(sub > s, column, 0.0)
+            bands[c] = bands[c] - column * scaled
+    out = []
+    for b in range(count):
+        diagonal = jnp.zeros((8, 1), jnp.float32)
+        for s in range(8):
+            diagonal = jnp.where(sub == s, pivots[8 * b + s], diagonal)
+        out.append(bands[b][:, size:] * lax.rsqrt(diagonal))
+    return jnp.concatenate(out, axis=0)
+
+
+def pack(gram):
+    half = gram.shape[0] // 2
+    return jnp.concatenate([gram[:half], gram[half:]], axis=1)
+
+
+def unpack(packed):
+    size = packed.shape[1] // 2
+    return jnp.concatenate([packed[:, :size], packed[:, size:]], axis=0)
+
+
+def ortho_kernel(plan, image_ref, scale_ref, out_ref, box, send_sem, recv_sem):
+    me = lax.axis_index(AXIS)
+    found = peers_of(me, plan)
+    barrier = pltpu.get_barrier_semaphore()
+    total = 0
+    for _, row in found:
+        for _, peer in row:
+            pl.semaphore_signal(barrier, inc=1, device_id={AXIS: peer}, device_id_type=MESH)
+            total += 1
+    normed = image_ref[...] * scale_ref[...]
+    gram = lax.dot_general(
+        normed, normed, (((0,), (0,)), ((), ())), precision=HIGH, preferred_element_type=jnp.float32
+    )
+    pl.semaphore_wait(barrier, total)
+    gram = unpack(all_sum(pack(gram), found, box, send_sem, recv_sem))
+    inverse = inverse_factor(gram)
+    out_ref[...] = lax.dot_general(
+        normed, inverse, (((1,), (1,)), ((), ())), precision=HIGH, preferred_element_type=jnp.float32
+    )
+
+
+def ortho(image, scale, peers):
+    size = image.shape[1]
+    plan = radices(peers)
+    return pl.pallas_call(
+        functools.partial(ortho_kernel, plan),
+        out_shape=jax.ShapeDtypeStruct(image.shape, jnp.float32),
+        in_specs=[pl.BlockSpec(memory_space=pltpu.VMEM)] * 2,
+        out_specs=pl.BlockSpec(memory_space=pltpu.VMEM),
+        scratch_shapes=[
+            pltpu.VMEM((len(plan), max(plan), size // 2, 2 * size), jnp.float32),
+            pltpu.SemaphoreType.DMA((len(plan), max(plan))),
+            pltpu.SemaphoreType.DMA((len(plan), max(plan))),
+        ],
+        compiler_params=pltpu.CompilerParams(collective_id=0, has_side_effects=True),
+        name="ortho",
+    )(image, scale)
 
 
 def shifted(array, axis, by):
@@ -35,7 +175,7 @@
     return jnp.concatenate(pieces, 0)
 
 
-def local(features, iterate, band_mask):
+def local(peers, features, iterate, band_mask):
     unit = unit_rows(features)
     keep_row = band_mask[0]
     reach = W
@@ -70,23 +210,13 @@
                 tiles[offset], scaled, (((0,), (0,)), ((), ())), preferred_element_type=jnp.float32
             )
             image = image + shifted(mirrored, "rows", offset)
-        normed = image * scale
-        local_gram = lax.dot_general(
-            normed,
-            normed,
-            (((0,), (0,)), ((), ())),
-            precision=lax.Precision.HIGHEST,
-            preferred_element_type=jnp.float32,
-        )
-        gram = lax.psum(local_gram, "rows")
-        lower = jnp.linalg.cholesky(gram)
-        current = jax.scipy.linalg.solve_triangular(lower, normed.T, lower=True).T
+        current = ortho(image, scale, peers)
     return (current, degrees)
 
 
 def solution(mesh):
     return jax.shard_map(
-        local,
+        functools.partial(local, mesh.shape[AXIS]),
         mesh=mesh,
         in_specs=(
             P(("groups", "rows"), None),

time: 226 us -> 156 us (0.69)
  blocking collectives: 121 us -> 0 us
  Pallas kernels: 0 us -> 47.8 us
  other arithmetic: 29.2 us -> 6.59 us
  matrix products: 18.5 us -> 28 us
  starting transfers between devices: 25.4 us -> 33.1 us
  local copies, waits for them, and re-layouts: 0.87 us -> 6.33 us
  waiting for transfers between devices: 29.1 us -> 32.3 us
    psum x2 -> x0, blocking collectives: 121 us -> none  [local(): gram = lax.psum(local_gram, 'rows')]
    pallas_call x0 -> x2, Pallas kernels: none -> 47.8 us  [ortho(): pl.pallas_call(functools.partial(ortho_kernel, plan), out_shape=jax.Shape...]
    another operation x11 -> x1, other arithmetic: 24.1 us -> 0.01 us  [the longest x6 13.1 us: local(): lower = jnp.linalg.cholesky(gram)]
    ppermute x12, starting transfers between devices: 25.4 us -> 33.1 us  [shifted(): return lax.ppermute(array, axis, pairs)]
    dot_general x4, matrix products: 5.45 us -> 12 us  [local(): jnp.dot(tiles[offset], neighbours[offset - 1], preferred_element_type=jnp...]
    dot_general x4, matrix products: 4.76 us -> 9.36 us  [local(): lax.dot_general(tiles[offset], scaled, (((0,), (0,)), ((), ())), preferre...]
    ppermute x12, waiting for transfers between devices: 29.1 us -> 32.3 us  [shifted(): return lax.ppermute(array, axis, pairs)]
    unnamed x18 -> x30, local copies, waits for them, and re-layouts: 0.09 us -> 2.41 us
  transfers between devices with their start and end apart: 12 -> 12, of which waited for: 4 -> 5; matrix products, arithmetic and copies ran while one was open for 5% -> 13% of each run, Pallas kernels for 0% -> 0%
where the time goes in v1:
time: 156 us; the launch traced here: 155 us
  Pallas kernels  47.8 us (31%)
  starting transfers between devices  33.1 us (21%)
  waiting for transfers between devices  32.3 us (21%)
  matrix products  28 us (18%)
  other arithmetic  6.59 us (4%)
  local copies, waits for them, and re-layouts  6.33 us (4%)
    pallas_call x2, Pallas kernels, ortho(): pl.pallas_call(functools.partial(ortho_kernel, plan), out_shape=jax.Shape...  47.8 us
    ppermute x12, starting transfers between devices, shifted(): return lax.ppermute(array, axis, pairs)  33.1 us
    ppermute x12, waiting for transfers between devices, shifted(): return lax.ppermute(array, axis, pairs)  32.3 us
    dot_general x4, matrix products, local(): jnp.dot(tiles[offset], neighbours[offset - 1], preferred_element_type=jnp...  12 us
    dot_general x4, matrix products, local(): lax.dot_general(tiles[offset], scaled, (((0,), (0,)), ((), ())), preferre...  9.36 us
    dot_general x6, matrix products, affinity(): lax.dot_general(left[start:start + step], right, (((1,), (1,)), ((), ()))...  4.47 us
  transfers between devices with their start and end apart: 12, of which 5 were waited for; matrix products, arithmetic and copies ran while one was open for 13% of the time, Pallas kernels for 0%

profile of v1, /device:TPU:0, one launch (start us, length us, event | category | flops | bytes accessed | tf_op | source)
XLA Modules:
  0.0 155.1 jit_solution(12410286731971337997)
XLA Ops:
  0.6 0.0 copy-start
  0.6 0.0 copy-start.13
  0.6 1.4 fusion
  2.1 0.2 fusion.1
  2.3 1.3 collective-permute-start.1
  3.6 1.3 collective-permute-start
  4.9 0.7 exponential_convert_fusion.4
  5.7 0.0 copy-start.6
  5.7 0.7 exponential_convert_fusion.5
  6.5 0.7 fusion.23
  7.2 17.6 %collective-permute-done.1 = bf16[1024,384]{1,0:T(8,128)(2,1)S(1)} collective-permute-done((bf16[1024,384]{1,0:T(8,128)(2,1)S(1)}, bf16[1024,384]{1,0:T(8,128)(2,1)S(1)}, u32[]{:S(2)}, u32[]{:S(2)}) %collective-permute-start.1) | collective-permute-done | bytes 786464 | tf_op jit(solution)/shard_map/ppermute | solution.py:153
  24.8 0.7 exponential_convert_fusion
  25.5 0.7 exponential_convert_fusion.1
  26.3 1.3 convert_reduce_fusion.1
  27.6 4.5 %collective-permute-start.3 = (f32[1024]{0:T(1024)S(1)}, f32[1024]{0:T(1024)S(1)}, u32[]{:S(2)}, u32[]{:S(2)}) collective-permute-start(f32[1024]{0:T(1024)S(1)} %get-tuple-element.11), channel_id=1, source_target_pairs={{0,2},{1,3},{2,4},{3,5},{4,6},{5,7},{6,8},{7,9},{8,10},{9,11},{10,... | collective-permute-start | bytes 12296 | tf_op jit(solution)/shard_map/ppermute | solution.py:153
  32.1 0.0 collective-permute-done
  32.1 0.7 exponential_convert_fusion.2
  32.9 0.0 copy-start.1
  32.9 0.7 exponential_convert_fusion.3
  33.6 0.2 copy-done.1
  33.9 1.3 convert_reduce_fusion.3
  35.1 0.0 copy-start.12
  35.2 2.9 %collective-permute-start.2 = (f32[1024]{0:T(1024)S(1)}, f32[1024]{0:T(1024)S(1)}, u32[]{:S(2)}, u32[]{:S(2)}) collective-permute-start(f32[1024]{0:T(1024)S(1)} %get-tuple-element.9), channel_id=1, source_target_pairs={{0,1},{1,2},{2,3},{3,4},{4,5},{5,6},{6,7},{7,8},{8,9},{9,10},{10,1... | collective-permute-start | bytes 12296 | tf_op jit(solution)/shard_map/ppermute | solution.py:153
  38.1 0.3 convert_reduce_fusion.4
  38.4 0.0 copy-done.12
  38.5 0.2 copy.31
  38.7 0.0 collective-permute-done.3
  38.7 0.2 collective-permute-done.2
  38.9 0.6 fusion.22
  39.5 0.2 multiply_convert_fusion.1
  39.7 2.4 %fusion.18 = f32[1024,64]{1,0:T(8,128)} fusion(bf16[1024,64]{1,0:T(8,128)(2,1)S(1)} %multiply_convert_fusion.1, bf16[512,1024]{1,0:T(8,128)(2,1)S(1)} %exponential_convert_fusion, bf16[512,1024]{1,0:T(8,128)(2,1)S(1)} %exponential_convert_fusion.1, bf16[]{:T(256)} %bitcast.1), kind=kOutput, calls=%fused_computation.41 | convolution fusion | flops 140509184 | bytes 2490370 | tf_op jit(solution)/shard_map/dot_general | solution.py:209
  42.1 0.0 copy-done.4
  42.1 2.4 %fusion.21 = f32[1024,64]{1,0:T(8,128)} fusion(bf16[1024,64]{1,0:T(8,128)(2,1)S(1)} %multiply_convert_fusion.1, bf16[512,1024]{1,0:T(8,128)(2,1)S(1)} %copy-done.2, bf16[512,1024]{1,0:T(8,128)(2,1)S(1)} %copy-done.4, bf16[]{:T(256)} %bitcast), kind=kOutput, calls=%fused_computation.44 | convolution fusion | flops 140509184 | bytes 2490370 | tf_op jit(solution)/shard_map/dot_general | solution.py:209
  44.5 1.3 collective-permute-start.4
  45.8 6.0 %collective-permute-start.7 = (f32[1024,64]{1,0:T(8,128)}, f32[1024,64]{1,0:T(8,128)}, u32[]{:S(2)}, u32[]{:S(2)}) collective-permute-start(f32[1024,64]{1,0:T(8,128)} %fusion.18), channel_id=1, source_target_pairs={{0,2},{1,3},{2,4},{3,5},{4,6},{5,7},{6,8},{7,9},{8,10},{9,11},{10,... | collective-permute-start | bytes 786440 | tf_op jit(solution)/shard_map/ppermute | solution.py:153
  51.8 2.9 %collective-permute-start.6 = (f32[1024,64]{1,0:T(8,128)}, f32[1024,64]{1,0:T(8,128)}, u32[]{:S(2)}, u32[]{:S(2)}) collective-permute-start(f32[1024,64]{1,0:T(8,128)} %fusion.21), channel_id=1, source_target_pairs={{0,1},{1,2},{2,3},{3,4},{4,5},{5,6},{6,7},{7,8},{8,9},{9,10},{10,1... | collective-permute-start | bytes 786440 | tf_op jit(solution)/shard_map/ppermute | solution.py:153
  54.8 1.5 fusion.7
  56.2 1.5 collective-permute-start.5
  57.7 1.0 copy.36.scale_ref
  58.8 0.0 collective-permute-done.4
  58.8 3.4 %convolution_add_fusion.2 = f32[1024,64]{0,1:T(8,128)} fusion(f32[1024,64]{0,1:T(8,128)} %fusion.7, bf16[1024,64]{1,0:T(8,128)(2,1)} %collective-permute-done.4, bf16[512,1024]{1,0:T(8,128)(2,1)S(1)} %copy-done.2, bf16[512,1024]{1,0:T(8,128)(2,1)} %copy-done.3, bf16[]{:T(256)} %bitcast), kind=kOutput, calls=%fused_computation.24 | convolution fusion | flops 140574720 | bytes 2752514 | tf_op jit(solution)/shard_map/dot_general | solution.py:205
  62.2 2.0 %copy.32 = f32[1024,64]{1,0:T(8,128)} copy(f32[1024,64]{0,1:T(8,128)} %convolution_add_fusion.2) | data formatting | bytes 524288 | tf_op jit(solution)/shard_map/add | solution.py:205
  64.2 2.9 %collective-permute-done.5 = bf16[1024,64]{1,0:T(8,128)(2,1)} collective-permute-done((bf16[1024,64]{1,0:T(8,128)(2,1)S(1)}, bf16[1024,64]{1,0:T(8,128)(2,1)}, u32[]{:S(2)}, u32[]{:S(2)}) %collective-permute-start.5) | collective-permute-done | bytes 131104 | tf_op jit(solution)/shard_map/ppermute | solution.py:153
  67.0 4.0 %collective-permute-done.7 = f32[1024,64]{1,0:T(8,128)} collective-permute-done((f32[1024,64]{1,0:T(8,128)}, f32[1024,64]{1,0:T(8,128)}, u32[]{:S(2)}, u32[]{:S(2)}) %collective-permute-start.7) | collective-permute-done | bytes 262176 | tf_op jit(solution)/shard_map/ppermute | solution.py:153
  71.0 0.0 collective-permute-done.6
  71.0 3.6 %fusion.5.image_ref = f32[1024,64]{1,0:T(8,128)} fusion(f32[1024,64]{1,0:T(8,128)} %collective-permute-done.7, f32[1024,64]{1,0:T(8,128)} %collective-permute-done.6, f32[1024,64]{1,0:T(8,128)} %copy.32, bf16[1024,64]{1,0:T(8,128)(2,1)} %collective-permute-done.5, bf16[512,1024]{1,0:T(8,128)(2,1)S(1)} %exponential_convert_fusion, ...), kind=kOutput, calls=%fused_computation.23 | convolution fusion | flops 140705792 | bytes 3276802 | tf_op jit(solution)/shard_map/dot_general | solution.py:205
  74.6 24.1 %ortho.2 = f32[1024,64]{1,0:T(8,128)} custom-call(f32[1024,64]{1,0:T(8,128)} %fusion.5.image_ref, f32[1024,1]{1,0:T(8,128)} %copy.36.scale_ref), custom_call_target="tpu_custom_call" | custom-call | tf_op jit(solution)/shard_map/ortho/pallas_call | solution.py:135
  98.8 1.2 multiply_convert_fusion
  100.0 2.3 %fusion.17 = f32[1024,64]{1,0:T(8,128)} fusion(bf16[1024,64]{1,0:T(8,128)(2,1)S(1)} %multiply_convert_fusion, bf16[512,1024]{1,0:T(8,128)(2,1)S(1)} %exponential_convert_fusion, bf16[512,1024]{1,0:T(8,128)(2,1)S(1)} %exponential_convert_fusion.1, bf16[]{:T(256)} %bitcast.1), kind=kOutput, calls=%fused_computation.40 | convolution fusion | flops 140509184 | bytes 2490370 | tf_op jit(solution)/shard_map/dot_general | solution.py:209
  102.3 1.3 collective-permute-start.8
  103.6 1.3 collective-permute-start.9
  104.9 5.3 %collective-permute-start.11 = (f32[1024,64]{1,0:T(8,128)}, f32[1024,64]{1,0:T(8,128)}, u32[]{:S(2)}, u32[]{:S(2)}) collective-permute-start(f32[1024,64]{1,0:T(8,128)} %fusion.17), channel_id=1, source_target_pairs={{0,2},{1,3},{2,4},{3,5},{4,6},{5,7},{6,8},{7,9},{8,10},{9,11},{10,... | collective-permute-start | bytes 786440 | tf_op jit(solution)/shard_map/ppermute | solution.py:153
  110.3 2.2 %fusion.19 = f32[1024,64]{1,0:T(8,128)} fusion(bf16[1024,64]{1,0:T(8,128)(2,1)S(1)} %multiply_convert_fusion, bf16[512,1024]{1,0:T(8,128)(2,1)S(1)} %copy-done.2, bf16[512,1024]{1,0:T(8,128)(2,1)S(1)} %copy-done.5, bf16[]{:T(256)} %bitcast), kind=kOutput, calls=%fused_computation.42 | convolution fusion | flops 140509184 | bytes 2490370 | tf_op jit(solution)/shard_map/dot_general | solution.py:209
  112.5 3.4 %collective-permute-start.10 = (f32[1024,64]{1,0:T(8,128)}, f32[1024,64]{1,0:T(8,128)}, u32[]{:S(2)}, u32[]{:S(2)}) collective-permute-start(f32[1024,64]{1,0:T(8,128)} %fusion.19), channel_id=1, source_target_pairs={{0,1},{1,2},{2,3},{3,4},{4,5},{5,6},{6,7},{7,8},{8,9},{9,10},{10,1... | collective-permute-start | bytes 786440 | tf_op jit(solution)/shard_map/ppermute | solution.py:153
  115.9 0.0 collective-permute-done.8
  115.9 1.4 fusion.20
  117.4 0.8 fusion.16
  118.1 0.2 copy.37
  118.3 0.0 collective-permute-done.9
  118.3 7.7 %collective-permute-done.11 = f32[1024,64]{1,0:T(8,128)} collective-permute-done((f32[1024,64]{1,0:T(8,128)}, f32[1024,64]{1,0:T(8,128)}, u32[]{:S(2)}, u32[]{:S(2)}) %collective-permute-start.11) | collective-permute-done | bytes 262176 | tf_op jit(solution)/shard_map/ppermute | solution.py:153
  126.0 0.0 collective-permute-done.10
  126.0 3.5 %fusion.3.image_ref = f32[1024,64]{1,0:T(8,128)} fusion(f32[1024,64]{1,0:T(8,128)} %collective-permute-done.11, f32[1024,64]{1,0:T(8,128)} %collective-permute-done.10, f32[1024,64]{1,0:T(8,128)S(1)} %copy.37, bf16[1024,64]{1,0:T(8,128)(2,1)} %collective-permute-done.9, bf16[512,1024]{1,0:T(8,128)(2,1)S(1)} %exponential_convert_fusion, ...), kind=kOutput, calls=%fused_computation.20 | convolution fusion | flops 140705792 | bytes 3276802 | tf_op jit(solution)/shard_map/dot_general | solution.py:205
  129.5 23.6 %ortho.3 = f32[1024,64]{1,0:T(8,128)} custom-call(f32[1024,64]{1,0:T(8,128)} %fusion.3.image_ref, f32[1024,1]{1,0:T(8,128)} %copy.36.scale_ref), custom_call_target="tpu_custom_call" | custom-call | tf_op jit(solution)/shard_map/ortho/pallas_call | solution.py:135
  153.2 1.9 %copy.42 = f32[1024,64]{0,1:T(8,128)} copy(f32[1024,64]{1,0:T(8,128)} %ortho.3) | data formatting | bytes 524288
  (22 shorter events, 0.0 us)
Async XLA Ops:
  0.6 1.5 copy-start
  0.6 4.3 %copy-start.13 = (s32[1,2]{1,0:T(1,128)S(1)}, s32[1,2]{1,0:T(1,128)}, u32[]{:S(2)}) copy-start(s32[1,2]{1,0:T(1,128)} %param.5) | copy-start | bytes 28
  2.3 22.4 %collective-permute-start.1 = (bf16[1024,384]{1,0:T(8,128)(2,1)S(1)}, bf16[1024,384]{1,0:T(8,128)(2,1)S(1)}, u32[]{:S(2)}, u32[]{:S(2)}) collective-permute-start(bf16[1024,384]{1,0:T(8,128)(2,1)S(1)} %fusion.1), channel_id=1, source_target_pairs={{2,0},{3,1},{4,2},{5,3},{6,4},{7,5},{8,6},{9,7},{10,8},{11,9},{12,... | collective-permute-start | bytes 2359304 | tf_op jit(solution)/shard_map/ppermute | solution.py:153
  3.6 28.5 %collective-permute-start = (bf16[1024,384]{1,0:T(8,128)(2,1)S(1)}, bf16[1024,384]{1,0:T(8,128)(2,1)S(1)}, u32[]{:S(2)}, u32[]{:S(2)}) collective-permute-start(bf16[1024,384]{1,0:T(8,128)(2,1)S(1)} %fusion.1), channel_id=1, source_target_pairs={{1,0},{2,1},{3,2},{4,3},{5,4},{6,5},{7,6},{8,7},{9,8},{10,9},{11,1... | collective-permute-start | bytes 2359304 | tf_op jit(solution)/shard_map/ppermute | solution.py:153
  5.7 32.4 %copy-start.6 = (bf16[512,1024]{1,0:T(8,128)(2,1)}, bf16[512,1024]{1,0:T(8,128)(2,1)S(1)}, u32[]{:S(2)}) copy-start(bf16[512,1024]{1,0:T(8,128)(2,1)S(1)} %exponential_convert_fusion.4) | copy-start | bytes 3145732
  6.5 31.6 %copy-start.9 = (bf16[512,1024]{1,0:T(8,128)(2,1)}, bf16[512,1024]{1,0:T(8,128)(2,1)S(1)}, u32[]{:S(2)}) copy-start(bf16[512,1024]{1,0:T(8,128)(2,1)S(1)} %exponential_convert_fusion.5) | copy-start | bytes 3145732
  27.6 11.1 %collective-permute-start.3 = (f32[1024]{0:T(1024)S(1)}, f32[1024]{0:T(1024)S(1)}, u32[]{:S(2)}, u32[]{:S(2)}) collective-permute-start(f32[1024]{0:T(1024)S(1)} %get-tuple-element.11), channel_id=1, source_target_pairs={{0,2},{1,3},{2,4},{3,5},{4,6},{5,7},{6,8},{7,9},{8,10},{9,11},{10,... | collective-permute-start | bytes 12296 | tf_op jit(solution)/shard_map/ppermute | solution.py:153
  32.9 1.0 copy-start.1
  33.6 1.5 copy-start.3
  35.1 3.3 %copy-start.12 = (f32[1024,64]{0,1:T(8,128)S(1)}, f32[1024,64]{0,1:T(8,128)}, u32[]{:S(2)}) copy-start(f32[1024,64]{0,1:T(8,128)} %param.4) | copy-start | bytes 786436
  35.2 3.7 %collective-permute-start.2 = (f32[1024]{0:T(1024)S(1)}, f32[1024]{0:T(1024)S(1)}, u32[]{:S(2)}, u32[]{:S(2)}) collective-permute-start(f32[1024]{0:T(1024)S(1)} %get-tuple-element.9), channel_id=1, source_target_pairs={{0,1},{1,2},{2,3},{3,4},{4,5},{5,6},{6,7},{7,8},{8,9},{9,10},{10,1... | collective-permute-start | bytes 12296 | tf_op jit(solution)/shard_map/ppermute | solution.py:153
  39.7 2.4 %copy-start.2 = (bf16[512,1024]{1,0:T(8,128)(2,1)S(1)}, bf16[512,1024]{1,0:T(8,128)(2,1)}, u32[]{:S(2)}) copy-start(bf16[512,1024]{1,0:T(8,128)(2,1)} %copy-done.1) | copy-start | bytes 3145732
  39.7 2.4 %copy-start.4 = (bf16[512,1024]{1,0:T(8,128)(2,1)S(1)}, bf16[512,1024]{1,0:T(8,128)(2,1)}, u32[]{:S(2)}) copy-start(bf16[512,1024]{1,0:T(8,128)(2,1)} %copy-done.3) | copy-start | bytes 3145732
  42.1 12.7 %copy-start.7 = (bf16[512,1024]{1,0:T(8,128)(2,1)S(1)}, bf16[512,1024]{1,0:T(8,128)(2,1)}, u32[]{:S(2)}) copy-start(bf16[512,1024]{1,0:T(8,128)(2,1)} %copy-done.6) | copy-start | bytes 3145732
  42.1 12.7 %copy-start.10 = (bf16[512,1024]{1,0:T(8,128)(2,1)S(1)}, bf16[512,1024]{1,0:T(8,128)(2,1)}, u32[]{:S(2)}) copy-start(bf16[512,1024]{1,0:T(8,128)(2,1)} %copy-done.9) | copy-start | bytes 3145732
  44.5 14.2 %collective-permute-start.4 = (bf16[1024,64]{1,0:T(8,128)(2,1)S(1)}, bf16[1024,64]{1,0:T(8,128)(2,1)}, u32[]{:S(2)}, u32[]{:S(2)}) collective-permute-start(bf16[1024,64]{1,0:T(8,128)(2,1)S(1)} %multiply_convert_fusion.1), channel_id=1, source_target_pairs={{1,0},{2,1},{3,2},{4,3},{5,4},{6,5},{7,6},{8,7},{9,8},{10,9},{11,1... | collective-permute-start | bytes 393224 | tf_op jit(solution)/shard_map/ppermute | solution.py:153
  45.8 25.2 %collective-permute-start.7 = (f32[1024,64]{1,0:T(8,128)}, f32[1024,64]{1,0:T(8,128)}, u32[]{:S(2)}, u32[]{:S(2)}) collective-permute-start(f32[1024,64]{1,0:T(8,128)} %fusion.18), channel_id=1, source_target_pairs={{0,2},{1,3},{2,4},{3,5},{4,6},{5,7},{6,8},{7,9},{8,10},{9,11},{10,... | collective-permute-start | bytes 786440 | tf_op jit(solution)/shard_map/ppermute | solution.py:153
  51.8 19.1 %collective-permute-start.6 = (f32[1024,64]{1,0:T(8,128)}, f32[1024,64]{1,0:T(8,128)}, u32[]{:S(2)}, u32[]{:S(2)}) collective-permute-start(f32[1024,64]{1,0:T(8,128)} %fusion.21), channel_id=1, source_target_pairs={{0,1},{1,2},{2,3},{3,4},{4,5},{5,6},{6,7},{7,8},{8,9},{9,10},{10,1... | collective-permute-start | bytes 786440 | tf_op jit(solution)/shard_map/ppermute | solution.py:153
  56.2 10.8 %collective-permute-start.5 = (bf16[1024,64]{1,0:T(8,128)(2,1)S(1)}, bf16[1024,64]{1,0:T(8,128)(2,1)}, u32[]{:S(2)}, u32[]{:S(2)}) collective-permute-start(bf16[1024,64]{1,0:T(8,128)(2,1)S(1)} %multiply_convert_fusion.1), channel_id=1, source_target_pairs={{2,0},{3,1},{4,2},{5,3},{6,4},{7,5},{8,6},{9,7},{10,8},{11,9},{12,... | collective-permute-start | bytes 393224 | tf_op jit(solution)/shard_map/ppermute | solution.py:153
  100.0 10.3 %copy-start.5 = (bf16[512,1024]{1,0:T(8,128)(2,1)S(1)}, bf16[512,1024]{1,0:T(8,128)(2,1)}, u32[]{:S(2)}) copy-start(bf16[512,1024]{1,0:T(8,128)(2,1)} %copy-done.3) | copy-start | bytes 3145732
  102.3 13.6 %collective-permute-start.8 = (bf16[1024,64]{1,0:T(8,128)(2,1)S(1)}, bf16[1024,64]{1,0:T(8,128)(2,1)S(1)}, u32[]{:S(2)}, u32[]{:S(2)}) collective-permute-start(bf16[1024,64]{1,0:T(8,128)(2,1)S(1)} %multiply_convert_fusion), channel_id=1, source_target_pairs={{1,0},{2,1},{3,2},{4,3},{5,4},{6,5},{7,6},{8,7},{9,8},{10,9},{11,1... | collective-permute-start | bytes 393224 | tf_op jit(solution)/shard_map/ppermute | solution.py:153
  103.6 14.7 %collective-permute-start.9 = (bf16[1024,64]{1,0:T(8,128)(2,1)S(1)}, bf16[1024,64]{1,0:T(8,128)(2,1)}, u32[]{:S(2)}, u32[]{:S(2)}) collective-permute-start(bf16[1024,64]{1,0:T(8,128)(2,1)S(1)} %multiply_convert_fusion), channel_id=1, source_target_pairs={{2,0},{3,1},{4,2},{5,3},{6,4},{7,5},{8,6},{9,7},{10,8},{11,9},{12,... | collective-permute-start | bytes 393224 | tf_op jit(solution)/shard_map/ppermute | solution.py:153
  104.9 21.1 %collective-permute-start.11 = (f32[1024,64]{1,0:T(8,128)}, f32[1024,64]{1,0:T(8,128)}, u32[]{:S(2)}, u32[]{:S(2)}) collective-permute-start(f32[1024,64]{1,0:T(8,128)} %fusion.17), channel_id=1, source_target_pairs={{0,2},{1,3},{2,4},{3,5},{4,6},{5,7},{6,8},{7,9},{8,10},{9,11},{10,... | collective-permute-start | bytes 786440 | tf_op jit(solution)/shard_map/ppermute | solution.py:153
  112.5 4.8 %copy-start.8 = (bf16[512,1024]{1,0:T(8,128)(2,1)S(1)}, bf16[512,1024]{1,0:T(8,128)(2,1)}, u32[]{:S(2)}) copy-start(bf16[512,1024]{1,0:T(8,128)(2,1)} %copy-done.6) | copy-start | bytes 3145732
  112.5 4.8 %copy-start.11 = (bf16[512,1024]{1,0:T(8,128)(2,1)S(1)}, bf16[512,1024]{1,0:T(8,128)(2,1)}, u32[]{:S(2)}) copy-start(bf16[512,1024]{1,0:T(8,128)(2,1)} %copy-done.9) | copy-start | bytes 3145732
  112.5 13.5 %collective-permute-start.10 = (f32[1024,64]{1,0:T(8,128)}, f32[1024,64]{1,0:T(8,128)}, u32[]{:S(2)}, u32[]{:S(2)}) collective-permute-start(f32[1024,64]{1,0:T(8,128)} %fusion.19), channel_id=1, source_target_pairs={{0,1},{1,2},{2,3},{3,4},{4,5},{5,6},{6,7},{7,8},{8,9},{9,10},{10,1... | collective-permute-start | bytes 786440 | tf_op jit(solution)/shard_map/ppermute | solution.py:153

commit v2 on v1

--- a/solution.py
+++ b/solution.py
@@ -108,7 +108,12 @@
     return jnp.concatenate([packed[:, :size], packed[:, size:]], axis=0)
 
 
-def ortho_kernel(plan, image_ref, scale_ref, out_ref, box, send_sem, recv_sem):
+def iterate_kernel(
+    plan, peers, current_ref, scale_ref, *refs
+):
+    tiles = refs[: W + 1]
+    out_ref, acc, p_send, p_recv, m_send, m_recv, box = refs[W + 1 : W + 8]
+    p_out, p_in, m_out, m_in, send_sem, recv_sem = refs[W + 8 :]
     me = lax.axis_index(AXIS)
     found = peers_of(me, plan)
     barrier = pltpu.get_barrier_semaphore()
@@ -117,34 +122,136 @@
         for _, peer in row:
             pl.semaphore_signal(barrier, inc=1, device_id={AXIS: peer}, device_id_type=MESH)
             total += 1
-    normed = image_ref[...] * scale_ref[...]
-    gram = lax.dot_general(
-        normed, normed, (((0,), (0,)), ((), ())), precision=HIGH, preferred_element_type=jnp.float32
-    )
+    for offset in range(1, W + 1):
+
+        @pl.when(me >= offset)
+        def _():
+            pl.semaphore_signal(barrier, inc=1, device_id={AXIS: me - offset}, device_id_type=MESH)
+
+        @pl.when(me + offset < peers)
+        def _():
+            pl.semaphore_signal(barrier, inc=1, device_id={AXIS: me + offset}, device_id_type=MESH)
+
+    for offset in range(1, W + 1):
+        total = total + (me >= offset).astype(jnp.int32) + (me + offset < peers).astype(jnp.int32)
     pl.semaphore_wait(barrier, total)
-    gram = unpack(all_sum(pack(gram), found, box, send_sem, recv_sem))
-    inverse = inverse_factor(gram)
-    out_ref[...] = lax.dot_general(
-        normed, inverse, (((1,), (1,)), ((), ())), precision=HIGH, preferred_element_type=jnp.float32
-    )
-
-
-def ortho(image, scale, peers):
-    size = image.shape[1]
+
+    def p_copy(step, offset, target):
+        return pltpu.make_async_remote_copy(
+            src_ref=p_send.at[step],
+            dst_ref=p_recv.at[step, offset - 1],
+            send_sem=p_out.at[step, offset - 1],
+            recv_sem=p_in.at[step, offset - 1],
+            device_id={AXIS: target},
+            device_id_type=MESH,
+        )
+
+    def m_copy(step, offset, target):
+        return pltpu.make_async_remote_copy(
+            src_ref=m_send.at[step, offset - 1],
+            dst_ref=m_recv.at[step, offset - 1],
+            send_sem=m_out.at[step, offset - 1],
+            recv_sem=m_in.at[step, offset - 1],
+            device_id={AXIS: target},
+            device_id_type=MESH,
+        )
+
+    scale = scale_ref[...]
+    out_ref[...] = current_ref[...]
+    for step in range(ITERS):
+        p_send[step] = (out_ref[...] * scale).astype(jnp.bfloat16)
+        for offset in range(1, W + 1):
+
+            @pl.when(me >= offset)
+            def _():
+                p_copy(step, offset, me - offset).start()
+
+        for offset in range(W, 0, -1):
+
+            @pl.when(me + offset < peers)
+            def _():
+                m_send[step, offset - 1] = lax.dot_general(
+                    p_send[step],
+                    tiles[offset][...],
+                    (((1,), (0,)), ((), ())),
+                    preferred_element_type=jnp.float32,
+                )
+                m_copy(step, offset, me + offset).start()
+
+        acc[...] = lax.dot_general(
+            p_send[step], tiles[0][...], (((1,), (1,)), ((), ())), preferred_element_type=jnp.float32
+        )
+        for offset in range(1, W + 1):
+
+            @pl.when(me + offset < peers)
+            def _():
+                p_copy(step, offset, me + offset).wait_recv()
+                acc[...] += lax.dot_general(
+                    p_recv[step, offset - 1],
+                    tiles[offset][...],
+                    (((1,), (1,)), ((), ())),
+                    preferred_element_type=jnp.float32,
+                )
+
+        for offset in range(1, W + 1):
+
+            @pl.when(me >= offset)
+            def _():
+                m_copy(step, offset, me - offset).wait_recv()
+                acc[...] += m_recv[step, offset - 1]
+
+        normed = acc[...] * scale
+        gram = lax.dot_general(
+            normed, normed, (((1,), (1,)), ((), ())), precision=HIGH, preferred_element_type=jnp.float32
+        )
+        gram = unpack(
+            all_sum(pack(gram), found, box.at[step], send_sem.at[step], recv_sem.at[step])
+        )
+        inverse = inverse_factor(gram)
+        out_ref[...] = lax.dot_general(
+            inverse, normed, (((1,), (0,)), ((), ())), precision=HIGH, preferred_element_type=jnp.float32
+        )
+    for step in range(ITERS):
+        for offset in range(1, W + 1):
+
+            @pl.when(me >= offset)
+            def _():
+                p_copy(step, offset, me - offset).wait_send()
+
+            @pl.when(me + offset < peers)
+            def _():
+                m_copy(step, offset, me + offset).wait_send()
+
+
+def iterations(current, scale, tiles, peers):
+    size, count = current.shape
     plan = radices(peers)
+    phases, widest = len(plan), max(plan)
+    dma = pltpu.SemaphoreType.DMA
     return pl.pallas_call(
-        functools.partial(ortho_kernel, plan),
-        out_shape=jax.ShapeDtypeStruct(image.shape, jnp.float32),
-        in_specs=[pl.BlockSpec(memory_space=pltpu.VMEM)] * 2,
+        functools.partial(iterate_kernel, plan, peers),
+        out_shape=jax.ShapeDtypeStruct(current.shape, jnp.float32),
+        in_specs=[pl.BlockSpec(memory_space=pltpu.VMEM)] * (W + 3),
         out_specs=pl.BlockSpec(memory_space=pltpu.VMEM),
         scratch_shapes=[
-            pltpu.VMEM((len(plan), max(plan), size // 2, 2 * size), jnp.float32),
-            pltpu.SemaphoreType.DMA((len(plan), max(plan))),
-            pltpu.SemaphoreType.DMA((len(plan), max(plan))),
+            pltpu.VMEM((size, count), jnp.float32),
+            pltpu.VMEM((ITERS, size, count), jnp.bfloat16),
+            pltpu.VMEM((ITERS, W, size, count), jnp.bfloat16),
+            pltpu.VMEM((ITERS, W, size, count), jnp.float32),
+            pltpu.VMEM((ITERS, W, size, count), jnp.float32),
+            pltpu.VMEM((ITERS, phases, widest, size // 2, 2 * size), jnp.float32),
+            dma((ITERS, W)),
+            dma((ITERS, W)),
+            dma((ITERS, W)),
+            dma((ITERS, W)),
+            dma((ITERS, phases, widest)),
+            dma((ITERS, phases, widest)),
         ],
-        compiler_params=pltpu.CompilerParams(collective_id=0, has_side_effects=True),
-        name="ortho",
-    )(image, scale)
+        compiler_params=pltpu.CompilerParams(
+            collective_id=0, has_side_effects=True, vmem_limit_bytes=48 << 20
+        ),
+        name="iterations",
+    )(current, scale, *tiles)
 
 
 def shifted(array, axis, by):
@@ -193,24 +300,8 @@
     for offset in range(1, reach + 1):
         column_sums = jnp.sum(tiles[offset].astype(jnp.float32), axis=0)
         degrees = degrees + shifted(column_sums, "rows", offset)
-    scale = lax.rsqrt(degrees)[:, None]
-    current = iterate
-    for step in range(ITERS):
-        scaled = (current * scale).astype(jnp.bfloat16)
-        neighbours = []
-        for offset in range(1, reach + 1):
-            neighbours.append(shifted(scaled, "rows", -offset))
-        image = jnp.dot(tiles[0], scaled, preferred_element_type=jnp.float32)
-        for offset in range(1, reach + 1):
-            image = image + jnp.dot(
-                tiles[offset], neighbours[offset - 1], preferred_element_type=jnp.float32
-            )
-        for offset in range(1, reach + 1):
-            mirrored = lax.dot_general(
-                tiles[offset], scaled, (((0,), (0,)), ((), ())), preferred_element_type=jnp.float32
-            )
-            image = image + shifted(mirrored, "rows", offset)
-        current = ortho(image, scale, peers)
+    scale = lax.rsqrt(degrees)[None, :]
+    current = iterations(iterate.T, scale, tiles, peers).T
     return (current, degrees)
 
 

time: 156 us -> 108 us (0.69)
  waiting for transfers between devices: 32.3 us -> 6.53 us
  matrix products: 28 us -> 4.48 us
  Pallas kernels: 47.8 us -> 61.2 us
  starting transfers between devices: 33.1 us -> 25.4 us
  local copies, waits for them, and re-layouts: 6.33 us -> 1.3 us
    ppermute x12 -> x4, waiting for transfers between devices: 32.3 us -> 6.53 us  [shifted(): return lax.ppermute(array, axis, pairs)]
    dot_general x10 -> x0, matrix products: 23.6 us -> none  [the longest x4 12 us: local(): jnp.dot(tiles[offset], neighbours[offset - 1], preferred_element_type=jnp...]
    pallas_call x2 -> x1, Pallas kernels: 47.8 us -> 61.2 us  [iterations(): pl.pallas_call(functools.partial(iterate_kernel, plan, peers), out_shape=...]
    ppermute x12 -> x4, starting transfers between devices: 33.1 us -> 25.4 us  [shifted(): return lax.ppermute(array, axis, pairs)]
    add x2 -> x0, local copies, waits for them, and re-layouts: 2.15 us -> none  [local(): image + jnp.dot(tiles[offset], neighbours[offset - 1], preferred_element_...]
    unnamed x30 -> x5, local copies, waits for them, and re-layouts: 2.41 us -> 0.71 us
  transfers between devices with their start and end apart: 12 -> 4, of which waited for: 5 -> 2; matrix products, arithmetic and copies ran while one was open for 13% -> 9% of each run, Pallas kernels for 0% -> 0%
where the time goes in v2:
time: 108 us
  Pallas kernels  61.2 us (57%)
  starting transfers between devices  25.4 us (24%)
  other arithmetic  7.82 us (7%)
  waiting for transfers between devices  6.53 us (6%)
  matrix products  4.48 us (4%)
  local copies, waits for them, and re-layouts  1.3 us (1%)
    pallas_call x1, Pallas kernels, iterations(): pl.pallas_call(functools.partial(iterate_kernel, plan, peers), out_shape=...  61.2 us
    ppermute x4, starting transfers between devices, shifted(): return lax.ppermute(array, axis, pairs)  25.4 us
    ppermute x4, waiting for transfers between devices, shifted(): return lax.ppermute(array, axis, pairs)  6.53 us
    dot_general x6, matrix products, affinity(): lax.dot_general(left[start:start + step], right, (((1,), (1,)), ((), ()))...  4.48 us
    reduce_sum x2, other arithmetic, local(): degrees = degrees + jnp.sum(tiles[offset].astype(jnp.float32), axis=1)  3.99 us
  transfers between devices with their start and end apart: 4, of which 2 were waited for; matrix products, arithmetic and copies ran while one was open for 9% of the time, Pallas kernels for 0%

profile of v2, /device:TPU:0, one launch (start us, length us, event | category | flops | bytes accessed | tf_op | source)
XLA Modules:
  0.0 107.5 jit_solution(1218422763252926155)
XLA Ops:
  0.6 0.0 copy-start.1
  0.6 1.4 %fusion = f32[1024]{0:T(1024)S(1)} fusion(bf16[1024,384]{1,0:T(8,128)(2,1)} %param.3), kind=kLoop, calls=%fused_computation.16 | loop fusion | flops 1178624 | bytes 790528 | tf_op jit(solution)/shard_map/reduce_sum | solution.py:265
  2.0 1.3 %fusion.1 = bf16[1024,384]{1,0:T(8,128)(2,1)S(1)} fusion(bf16[1024,384]{1,0:T(8,128)(2,1)} %param.3, f32[1024]{0:T(1024)S(1)} %add_rsqrt_fusion), kind=kLoop, calls=%fused_computation.17 | loop fusion | flops 1179648 | bytes 1576960 | tf_op jit(solution)/shard_map/convert_element_type | solution.py:265
  3.4 1.3 %collective-permute-start = (bf16[1024,384]{1,0:T(8,128)(2,1)S(1)}, bf16[1024,384]{1,0:T(8,128)(2,1)S(1)}, u32[]{:S(2)}, u32[]{:S(2)}) collective-permute-start(bf16[1024,384]{1,0:T(8,128)(2,1)S(1)} %fusion.1), channel_id=1, source_target_pairs={{1,0},{2,1},{3,2},{4,3},{5,4},{6,5},{7,6},{8,7},{9,8},{10,9},{11,1... | collective-permute-start | bytes 2359304 | tf_op jit(solution)/shard_map/ppermute | solution.py:260
  4.7 1.3 %collective-permute-start.1 = (bf16[1024,384]{1,0:T(8,128)(2,1)S(1)}, bf16[1024,384]{1,0:T(8,128)(2,1)S(1)}, u32[]{:S(2)}, u32[]{:S(2)}) collective-permute-start(bf16[1024,384]{1,0:T(8,128)(2,1)S(1)} %fusion.1), channel_id=1, source_target_pairs={{2,0},{3,1},{4,2},{5,3},{6,4},{7,5},{8,6},{9,7},{10,8},{11,9},{12,... | collective-permute-start | bytes 2359304 | tf_op jit(solution)/shard_map/ppermute | solution.py:260
  6.0 0.0 copy-done.1
  6.0 0.7 exponential_convert_fusion.4
  6.7 0.7 exponential_convert_fusion.5
  7.5 0.2 pad_maximum_fusion.refs_0_
  7.7 0.6 fusion.9
  8.3 0.0 collective-permute-done
  8.3 0.7 exponential_convert_fusion.2
  9.0 0.7 exponential_convert_fusion.3
  9.8 1.4 %convert_reduce_fusion.3 = (f32[1024]{0:T(1024)S(1)}, f32[1024]{0:T(1024)S(1)}, bf16[1024,1024]{1,0:T(8,128)(2,1)S(1)}) fusion(bf16[]{:T(256)} %bitcast.1, bf16[512,1024]{1,0:T(8,128)(2,1)S(1)} %exponential_convert_fusion.2, bf16[512,1024]{1,0:T(8,128)(2,1)S(1)} %exponential_convert_fusion.3), kind=kLoop, calls=%fused_computation.3 | loop fusion | flops 9435136 | bytes 4202498 | tf_op jit(solution)/shard_map/reduce_sum | solution.py:299
  11.1 18.4 %collective-permute-start.2 = (f32[1024]{0:T(1024)S(1)}, f32[1024]{0:T(1024)S(1)}, u32[]{:S(2)}, u32[]{:S(2)}) collective-permute-start(f32[1024]{0:T(1024)S(1)} %get-tuple-element.3), channel_id=1, source_target_pairs={{0,1},{1,2},{2,3},{3,4},{4,5},{5,6},{6,7},{7,8},{8,9},{9,10},{10,1... | collective-permute-start | bytes 12296 | tf_op jit(solution)/shard_map/ppermute | solution.py:260
  29.5 5.6 %collective-permute-done.1 = bf16[1024,384]{1,0:T(8,128)(2,1)S(1)} collective-permute-done((bf16[1024,384]{1,0:T(8,128)(2,1)S(1)}, bf16[1024,384]{1,0:T(8,128)(2,1)S(1)}, u32[]{:S(2)}, u32[]{:S(2)}) %collective-permute-start.1) | collective-permute-done | bytes 786464 | tf_op jit(solution)/shard_map/ppermute | solution.py:260
  35.1 0.7 exponential_convert_fusion.1
  35.8 0.7 exponential_convert_fusion
  36.6 2.6 %convert_reduce_fusion.1 = (f32[1024]{0:T(1024)S(1)}, f32[1024]{0:T(1024)S(1)}, bf16[1024,1024]{1,0:T(8,128)(2,1)}) fusion(bf16[]{:T(256)} %bitcast.2, bf16[512,1024]{1,0:T(8,128)(2,1)S(1)} %exponential_convert_fusion, bf16[512,1024]{1,0:T(8,128)(2,1)S(1)} %exponential_convert_fusion.1), kind=kLoop, calls=%fused_computation.1 | loop fusion | flops 9435136 | bytes 4202498 | tf_op jit(solution)/shard_map/reduce_sum | solution.py:299
  39.2 0.0 copy-start
  39.2 4.4 %collective-permute-start.3 = (f32[1024]{0:T(1024)S(1)}, f32[1024]{0:T(1024)S(1)}, u32[]{:S(2)}, u32[]{:S(2)}) collective-permute-start(f32[1024]{0:T(1024)S(1)} %get-tuple-element.5), channel_id=1, source_target_pairs={{0,2},{1,3},{2,4},{3,5},{4,6},{5,7},{6,8},{7,9},{8,10},{9,11},{10,... | collective-permute-start | bytes 12296 | tf_op jit(solution)/shard_map/ppermute | solution.py:260
  43.7 0.3 convert_reduce_fusion.4
  44.0 0.0 collective-permute-done.2
  44.0 1.0 collective-permute-done.3
  45.0 0.6 fusion.8
  45.6 0.0 copy-done
  45.6 61.2 %iterations.1 = f32[64,1024]{1,0:T(8,128)S(1)} custom-call(f32[64,1024]{1,0:T(8,128)S(1)} %bitcast.12, f32[1,1024]{1,0:T(1,128)S(1)} %bitcast.13, bf16[1024,1024]{1,0:T(8,128)(2,1)S(1)} %pad_maximum_fusion.refs_0_, bf16[1024,1024]{1,0:T(8,128)(2,1)S(1)} %get-tuple-element.8.refs_1_, bf16[1024,1024]{1,0:T(8,128)(2,1)} %get-tuple-element.9.refs_2_), custom_call_target="tpu_custom_call" | custom-call | tf_op jit(solution)/shard_map/iterations/pallas_call | solution.py:231
  106.8 0.7 copy.6
  (2 shorter events, 0.0 us)
Async XLA Ops:
  0.6 5.3 %copy-start.1 = (s32[1,2]{1,0:T(1,128)S(1)}, s32[1,2]{1,0:T(1,128)}, u32[]{:S(2)}) copy-start(s32[1,2]{1,0:T(1,128)} %param.5) | copy-start | bytes 28
  3.4 4.9 %collective-permute-start = (bf16[1024,384]{1,0:T(8,128)(2,1)S(1)}, bf16[1024,384]{1,0:T(8,128)(2,1)S(1)}, u32[]{:S(2)}, u32[]{:S(2)}) collective-permute-start(bf16[1024,384]{1,0:T(8,128)(2,1)S(1)} %fusion.1), channel_id=1, source_target_pairs={{1,0},{2,1},{3,2},{4,3},{5,4},{6,5},{7,6},{8,7},{9,8},{10,9},{11,1... | collective-permute-start | bytes 2359304 | tf_op jit(solution)/shard_map/ppermute | solution.py:260
  4.7 30.4 %collective-permute-start.1 = (bf16[1024,384]{1,0:T(8,128)(2,1)S(1)}, bf16[1024,384]{1,0:T(8,128)(2,1)S(1)}, u32[]{:S(2)}, u32[]{:S(2)}) collective-permute-start(bf16[1024,384]{1,0:T(8,128)(2,1)S(1)} %fusion.1), channel_id=1, source_target_pairs={{2,0},{3,1},{4,2},{5,3},{6,4},{7,5},{8,6},{9,7},{10,8},{11,9},{12,... | collective-permute-start | bytes 2359304 | tf_op jit(solution)/shard_map/ppermute | solution.py:260
  11.1 32.9 %collective-permute-start.2 = (f32[1024]{0:T(1024)S(1)}, f32[1024]{0:T(1024)S(1)}, u32[]{:S(2)}, u32[]{:S(2)}) collective-permute-start(f32[1024]{0:T(1024)S(1)} %get-tuple-element.3), channel_id=1, source_target_pairs={{0,1},{1,2},{2,3},{3,4},{4,5},{5,6},{6,7},{7,8},{8,9},{9,10},{10,1... | collective-permute-start | bytes 12296 | tf_op jit(solution)/shard_map/ppermute | solution.py:260
  39.2 6.3 %copy-start = (f32[1024,64]{0,1:T(8,128)S(1)}, f32[1024,64]{0,1:T(8,128)}, u32[]{:S(2)}) copy-start(f32[1024,64]{0,1:T(8,128)} %param.4) | copy-start | bytes 786436
  39.2 5.7 %collective-permute-start.3 = (f32[1024]{0:T(1024)S(1)}, f32[1024]{0:T(1024)S(1)}, u32[]{:S(2)}, u32[]{:S(2)}) collective-permute-start(f32[1024]{0:T(1024)S(1)} %get-tuple-element.5), channel_id=1, source_target_pairs={{0,2},{1,3},{2,4},{3,5},{4,6},{5,7},{6,8},{7,9},{8,10},{9,11},{10,... | collective-permute-start | bytes 12296 | tf_op jit(solution)/shard_map/ppermute | solution.py:260

commit v3 on v2

--- a/solution.py
+++ b/solution.py
@@ -78,17 +78,23 @@
     bands = [both[8 * b : 8 * b + 8] for b in range(count)]
     sub = lax.broadcasted_iota(jnp.int32, (8, 1), 0)
     pivots = []
-    for j in range(size):
+    for j in range(0, size, 2):
         b, s = j // 8, j % 8
-        row = bands[b][s : s + 1]
-        pivot = row[:, j : j + 1]
-        pivots.append(pivot)
-        scaled = row * (1.0 / pivot)
+        first, second = bands[b][s : s + 1], bands[b][s + 1 : s + 2]
+        pivot = first[:, j : j + 1]
+        first_scaled = first * (1.0 / pivot)
+        reduced = second - second[:, j : j + 1] * first_scaled
+        after = reduced[:, j + 1 : j + 2]
+        second_scaled = reduced * (1.0 / after)
+        coupling = first_scaled[:, j + 1 : j + 2]
+        pivots += [pivot, after]
         for c in range(b, count):
-            column = bands[c][:, j : j + 1]
+            left = bands[c][:, j : j + 1]
+            right = bands[c][:, j + 1 : j + 2] - left * coupling
             if c == b:
-                column = jnp.where(sub > s, column, 0.0)
-            bands[c] = bands[c] - column * scaled
+                left = jnp.where(sub > s, left, 0.0)
+                right = jnp.where(sub > s + 1, right, 0.0)
+            bands[c] = bands[c] - left * first_scaled - right * second_scaled
     out = []
     for b in range(count):
         diagonal = jnp.zeros((8, 1), jnp.float32)
@@ -286,9 +292,10 @@
     unit = unit_rows(features)
     keep_row = band_mask[0]
     reach = W
-    partners = []
-    for offset in range(1, reach + 1):
-        partners.append(shifted(unit, "rows", -offset))
+    nearest = shifted(unit, "rows", -1)
+    direct = lax.ppermute(unit, "rows", [(i + 2, i) for i in range(1, peers - 2, 2)])
+    relayed = lax.ppermute(nearest, "rows", [(i + 1, i) for i in range(0, peers - 2, 2)])
+    partners = [nearest, jnp.where(lax.rem(lax.axis_index("rows"), 2) == 0, relayed, direct)]
     tiles = [affinity(unit, unit)]
     for offset in range(1, reach + 1):
         keep = keep_row[offset - 1]

time: 108 us -> 111 us (1.028)
  Pallas kernels: 61.2 us -> 68.3 us
  waiting for transfers between devices: 6.53 us -> 1.41 us
    pallas_call x1, Pallas kernels: 61.2 us -> 68.3 us  [iterations(): pl.pallas_call(functools.partial(iterate_kernel, plan, peers), out_shape=...]
    ppermute x4 -> x3, waiting for transfers between devices: 6.53 us -> 1.4 us  [shifted(): return lax.ppermute(array, axis, pairs)]
    ppermute x0 -> x2, starting transfers between devices: none -> 1.99 us  [the longest x1 1.28 us: local(): lax.ppermute(nearest, 'rows', [(i + 1, i) for i in range(0, peers - 2, 2)])]
    ppermute x4 -> x3, starting transfers between devices: 25.4 us -> 24.5 us  [shifted(): return lax.ppermute(array, axis, pairs)]
  transfers between devices with their start and end apart: 4 -> 5, of which waited for: 2 -> 2; matrix products, arithmetic and copies ran while one was open for 9% -> 9% of each run, Pallas kernels for 0% -> 0%
where the time goes in v3:
time: 111 us
  Pallas kernels  68.3 us (62%)
  starting transfers between devices  26.5 us (24%)
  other arithmetic  7.82 us (7%)
  matrix products  4.49 us (4%)
  waiting for transfers between devices  1.41 us (1%)
  local copies, waits for them, and re-layouts  1.3 us (1%)
    pallas_call x1, Pallas kernels, iterations(): pl.pallas_call(functools.partial(iterate_kernel, plan, peers), out_shape=...  68.3 us
    ppermute x3, starting transfers between devices, shifted(): return lax.ppermute(array, axis, pairs)  24.5 us
    dot_general x6, matrix products, affinity(): lax.dot_general(left[start:start + step], right, (((1,), (1,)), ((), ()))...  4.49 us
    reduce_sum x2, other arithmetic, local(): degrees = degrees + jnp.sum(tiles[offset].astype(jnp.float32), axis=1)  3.99 us
  transfers between devices with their start and end apart: 5, of which 2 were waited for; matrix products, arithmetic and copies ran while one was open for 9% of the time, Pallas kernels for 0%

profile of v3, /device:TPU:0, one launch (start us, length us, event | category | flops | bytes accessed | tf_op | source)
XLA Modules:
  0.0 110.7 jit_solution(16824938045612329219)
XLA Ops:
  0.6 0.0 copy-start.1
  0.6 1.4 %fusion = f32[1024]{0:T(1024)S(1)} fusion(bf16[1024,384]{1,0:T(8,128)(2,1)} %param.3), kind=kLoop, calls=%fused_computation.16 | loop fusion | flops 1178624 | bytes 790528 | tf_op jit(solution)/shard_map/reduce_sum | solution.py:271
  2.0 1.3 %fusion.1 = bf16[1024,384]{1,0:T(8,128)(2,1)S(1)} fusion(bf16[1024,384]{1,0:T(8,128)(2,1)} %param.3, f32[1024]{0:T(1024)S(1)} %add_rsqrt_fusion), kind=kLoop, calls=%fused_computation.17 | loop fusion | flops 1179648 | bytes 1576960 | tf_op jit(solution)/shard_map/convert_element_type | solution.py:271
  3.4 1.3 %collective-permute-start = (bf16[1024,384]{1,0:T(8,128)(2,1)S(1)}, bf16[1024,384]{1,0:T(8,128)(2,1)S(1)}, u32[]{:S(2)}, u32[]{:S(2)}) collective-permute-start(bf16[1024,384]{1,0:T(8,128)(2,1)S(1)} %fusion.1), channel_id=1, source_target_pairs={{1,0},{2,1},{3,2},{4,3},{5,4},{6,5},{7,6},{8,7},{9,8},{10,9},{11,1... | collective-permute-start | bytes 2359304 | tf_op jit(solution)/shard_map/ppermute | solution.py:266
  4.7 0.7 collective-permute-start.2
  5.4 0.0 copy-done.1
  5.4 0.7 exponential_convert_fusion.4
  6.2 0.7 exponential_convert_fusion.5
  6.9 0.2 pad_maximum_fusion.refs_0_
  7.1 0.4 collective-permute-done
  7.5 1.3 %collective-permute-start.1 = (bf16[1024,384]{1,0:T(8,128)(2,1)S(1)}, bf16[1024,384]{1,0:T(8,128)(2,1)S(1)}, u32[]{:S(2)}, u32[]{:S(2)}) collective-permute-start(bf16[1024,384]{1,0:T(8,128)(2,1)S(1)} %collective-permute-done), channel_id=1, source_target_pairs={{1,0},{3,2},{5,4},{7,6},{9,8},{11,10},{13,12},{17,16},{19,18},{21,... | collective-permute-start | bytes 2359304 | tf_op jit(solution)/shard_map/ppermute | solution.py:297
  8.8 0.6 fusion.9
  9.4 0.7 exponential_convert_fusion.2
  10.2 0.7 exponential_convert_fusion.3
  10.9 1.4 %convert_reduce_fusion.3 = (f32[1024]{0:T(1024)S(1)}, f32[1024]{0:T(1024)S(1)}, bf16[1024,1024]{1,0:T(8,128)(2,1)S(1)}) fusion(bf16[]{:T(256)} %bitcast.1, bf16[512,1024]{1,0:T(8,128)(2,1)S(1)} %exponential_convert_fusion.2, bf16[512,1024]{1,0:T(8,128)(2,1)S(1)} %exponential_convert_fusion.3), kind=kLoop, calls=%fused_computation.3 | loop fusion | flops 9435136 | bytes 4202498 | tf_op jit(solution)/shard_map/reduce_sum | solution.py:306
  12.3 19.1 %collective-permute-start.3 = (f32[1024]{0:T(1024)S(1)}, f32[1024]{0:T(1024)S(1)}, u32[]{:S(2)}, u32[]{:S(2)}) collective-permute-start(f32[1024]{0:T(1024)S(1)} %get-tuple-element.3), channel_id=1, source_target_pairs={{0,1},{1,2},{2,3},{3,4},{4,5},{5,6},{6,7},{7,8},{8,9},{9,10},{10,1... | collective-permute-start | bytes 12296 | tf_op jit(solution)/shard_map/ppermute | solution.py:266
  31.4 0.0 collective-permute-done.2
  31.4 0.0 collective-permute-done.1
  31.4 0.8 exponential_convert_fusion.1
  32.2 0.8 exponential_convert_fusion
  33.0 2.6 %convert_reduce_fusion.1 = (f32[1024]{0:T(1024)S(1)}, f32[1024]{0:T(1024)S(1)}, bf16[1024,1024]{1,0:T(8,128)(2,1)}) fusion(bf16[]{:T(256)} %bitcast.2, bf16[512,1024]{1,0:T(8,128)(2,1)S(1)} %exponential_convert_fusion, bf16[512,1024]{1,0:T(8,128)(2,1)S(1)} %exponential_convert_fusion.1), kind=kLoop, calls=%fused_computation.1 | loop fusion | flops 9435136 | bytes 4202498 | tf_op jit(solution)/shard_map/reduce_sum | solution.py:306
  35.6 0.0 copy-start
  35.6 4.1 %collective-permute-start.4 = (f32[1024]{0:T(1024)S(1)}, f32[1024]{0:T(1024)S(1)}, u32[]{:S(2)}, u32[]{:S(2)}) collective-permute-start(f32[1024]{0:T(1024)S(1)} %get-tuple-element.5), channel_id=1, source_target_pairs={{0,2},{1,3},{2,4},{3,5},{4,6},{5,7},{6,8},{7,9},{8,10},{9,11},{10,... | collective-permute-start | bytes 12296 | tf_op jit(solution)/shard_map/ppermute | solution.py:266
  39.7 0.3 convert_reduce_fusion.4
  40.1 0.0 collective-permute-done.3
  40.1 1.0 collective-permute-done.4
  41.0 0.6 fusion.8
  41.6 0.0 copy-done
  41.6 68.3 %iterations.1 = f32[64,1024]{1,0:T(8,128)S(1)} custom-call(f32[64,1024]{1,0:T(8,128)S(1)} %bitcast.10, f32[1,1024]{1,0:T(1,128)S(1)} %bitcast.11, bf16[1024,1024]{1,0:T(8,128)(2,1)S(1)} %pad_maximum_fusion.refs_0_, bf16[1024,1024]{1,0:T(8,128)(2,1)S(1)} %get-tuple-element.8.refs_1_, bf16[1024,1024]{1,0:T(8,128)(2,1)} %get-tuple-element.9.refs_2_), custom_call_target="tpu_custom_call" | custom-call | tf_op jit(solution)/shard_map/iterations/pallas_call | solution.py:237
  110.0 0.7 copy.6
  (2 shorter events, 0.0 us)
Async XLA Ops:
  0.6 4.8 %copy-start.1 = (s32[1,2]{1,0:T(1,128)S(1)}, s32[1,2]{1,0:T(1,128)}, u32[]{:S(2)}) copy-start(s32[1,2]{1,0:T(1,128)} %param.5) | copy-start | bytes 28
  3.4 4.2 %collective-permute-start = (bf16[1024,384]{1,0:T(8,128)(2,1)S(1)}, bf16[1024,384]{1,0:T(8,128)(2,1)S(1)}, u32[]{:S(2)}, u32[]{:S(2)}) collective-permute-start(bf16[1024,384]{1,0:T(8,128)(2,1)S(1)} %fusion.1), channel_id=1, source_target_pairs={{1,0},{2,1},{3,2},{4,3},{5,4},{6,5},{7,6},{8,7},{9,8},{10,9},{11,1... | collective-permute-start | bytes 2359304 | tf_op jit(solution)/shard_map/ppermute | solution.py:266
  4.7 26.8 %collective-permute-start.2 = (bf16[1024,384]{1,0:T(8,128)(2,1)S(1)}, bf16[1024,384]{1,0:T(8,128)(2,1)S(1)}, u32[]{:S(2)}, u32[]{:S(2)}) collective-permute-start(bf16[1024,384]{1,0:T(8,128)(2,1)S(1)} %fusion.1), channel_id=1, source_target_pairs={{3,1},{5,3},{7,5},{9,7},{11,9},{13,11},{15,13},{19,17},{21,19},{23... | collective-permute-start | bytes 2359304 | tf_op jit(solution)/shard_map/ppermute | solution.py:296
  7.5 23.9 %collective-permute-start.1 = (bf16[1024,384]{1,0:T(8,128)(2,1)S(1)}, bf16[1024,384]{1,0:T(8,128)(2,1)S(1)}, u32[]{:S(2)}, u32[]{:S(2)}) collective-permute-start(bf16[1024,384]{1,0:T(8,128)(2,1)S(1)} %collective-permute-done), channel_id=1, source_target_pairs={{1,0},{3,2},{5,4},{7,6},{9,8},{11,10},{13,12},{17,16},{19,18},{21,... | collective-permute-start | bytes 2359304 | tf_op jit(solution)/shard_map/ppermute | solution.py:297
  12.3 27.8 %collective-permute-start.3 = (f32[1024]{0:T(1024)S(1)}, f32[1024]{0:T(1024)S(1)}, u32[]{:S(2)}, u32[]{:S(2)}) collective-permute-start(f32[1024]{0:T(1024)S(1)} %get-tuple-element.3), channel_id=1, source_target_pairs={{0,1},{1,2},{2,3},{3,4},{4,5},{5,6},{6,7},{7,8},{8,9},{9,10},{10,1... | collective-permute-start | bytes 12296 | tf_op jit(solution)/shard_map/ppermute | solution.py:266
  35.6 6.0 %copy-start = (f32[1024,64]{0,1:T(8,128)S(1)}, f32[1024,64]{0,1:T(8,128)}, u32[]{:S(2)}) copy-start(f32[1024,64]{0,1:T(8,128)} %param.4) | copy-start | bytes 786436
  35.6 5.4 %collective-permute-start.4 = (f32[1024]{0:T(1024)S(1)}, f32[1024]{0:T(1024)S(1)}, u32[]{:S(2)}, u32[]{:S(2)}) collective-permute-start(f32[1024]{0:T(1024)S(1)} %get-tuple-element.5), channel_id=1, source_target_pairs={{0,2},{1,3},{2,4},{3,5},{4,6},{5,7},{6,8},{7,9},{8,10},{9,11},{10,... | collective-permute-start | bytes 12296 | tf_op jit(solution)/shard_map/ppermute | solution.py:266

commit v4 on v2

--- a/solution.py
+++ b/solution.py
@@ -286,9 +286,10 @@
     unit = unit_rows(features)
     keep_row = band_mask[0]
     reach = W
-    partners = []
-    for offset in range(1, reach + 1):
-        partners.append(shifted(unit, "rows", -offset))
+    nearest = shifted(unit, "rows", -1)
+    direct = lax.ppermute(unit, "rows", [(i + 2, i) for i in range(1, peers - 2, 2)])
+    relayed = lax.ppermute(nearest, "rows", [(i + 1, i) for i in range(0, peers - 2, 2)])
+    partners = [nearest, jnp.where(lax.rem(lax.axis_index("rows"), 2) == 0, relayed, direct)]
     tiles = [affinity(unit, unit)]
     for offset in range(1, reach + 1):
         keep = keep_row[offset - 1]

time: 108 us -> 104 us (0.963)
  waiting for transfers between devices: 6.53 us -> 1.4 us
  starting transfers between devices: 25.4 us -> 26.5 us
    ppermute x4 -> x3, waiting for transfers between devices: 6.53 us -> 1.4 us  [shifted(): return lax.ppermute(array, axis, pairs)]
    ppermute x0 -> x2, starting transfers between devices: none -> 1.99 us  [the longest x1 1.28 us: local(): lax.ppermute(nearest, 'rows', [(i + 1, i) for i in range(0, peers - 2, 2)])]
    ppermute x4 -> x3, starting transfers between devices: 25.4 us -> 24.5 us  [shifted(): return lax.ppermute(array, axis, pairs)]
  transfers between devices with their start and end apart: 4 -> 5, of which waited for: 2 -> 2; matrix products, arithmetic and copies ran while one was open for 9% -> 9% of each run, Pallas kernels for 0% -> 0%
where the time goes in v4:
time: 104 us; the launch traced here: 103 us
  Pallas kernels  61.1 us (59%)
  starting transfers between devices  26.5 us (25%)
  other arithmetic  7.82 us (8%)
  matrix products  4.51 us (4%)
  waiting for transfers between devices  1.4 us (1%)
  local copies, waits for them, and re-layouts  1.3 us (1%)
    pallas_call x1, Pallas kernels, iterations(): pl.pallas_call(functools.partial(iterate_kernel, plan, peers), out_shape=...  61.1 us
    ppermute x3, starting transfers between devices, shifted(): return lax.ppermute(array, axis, pairs)  24.5 us
    dot_general x6, matrix products, affinity(): lax.dot_general(left[start:start + step], right, (((1,), (1,)), ((), ()))...  4.51 us
    reduce_sum x2, other arithmetic, local(): degrees = degrees + jnp.sum(tiles[offset].astype(jnp.float32), axis=1)  3.99 us
  transfers between devices with their start and end apart: 5, of which 2 were waited for; matrix products, arithmetic and copies ran while one was open for 9% of the time, Pallas kernels for 0%

profile of v4, /device:TPU:0, one launch (start us, length us, event | category | flops | bytes accessed | tf_op | source)
XLA Modules:
  0.0 103.4 jit_solution(10271339832094329817)
XLA Ops:
  0.6 0.0 copy-start.1
  0.6 1.4 %fusion = f32[1024]{0:T(1024)S(1)} fusion(bf16[1024,384]{1,0:T(8,128)(2,1)} %param.3), kind=kLoop, calls=%fused_computation.16 | loop fusion | flops 1178624 | bytes 790528 | tf_op jit(solution)/shard_map/reduce_sum | solution.py:265
  2.0 1.3 %fusion.1 = bf16[1024,384]{1,0:T(8,128)(2,1)S(1)} fusion(bf16[1024,384]{1,0:T(8,128)(2,1)} %param.3, f32[1024]{0:T(1024)S(1)} %add_rsqrt_fusion), kind=kLoop, calls=%fused_computation.17 | loop fusion | flops 1179648 | bytes 1576960 | tf_op jit(solution)/shard_map/convert_element_type | solution.py:265
  3.4 1.3 %collective-permute-start = (bf16[1024,384]{1,0:T(8,128)(2,1)S(1)}, bf16[1024,384]{1,0:T(8,128)(2,1)S(1)}, u32[]{:S(2)}, u32[]{:S(2)}) collective-permute-start(bf16[1024,384]{1,0:T(8,128)(2,1)S(1)} %fusion.1), channel_id=1, source_target_pairs={{1,0},{2,1},{3,2},{4,3},{5,4},{6,5},{7,6},{8,7},{9,8},{10,9},{11,1... | collective-permute-start | bytes 2359304 | tf_op jit(solution)/shard_map/ppermute | solution.py:260
  4.7 0.7 collective-permute-start.2
  5.4 0.0 copy-done.1
  5.4 0.7 exponential_convert_fusion.4
  6.2 0.8 exponential_convert_fusion.5
  6.9 0.2 pad_maximum_fusion.refs_0_
  7.1 0.4 collective-permute-done
  7.5 1.3 %collective-permute-start.1 = (bf16[1024,384]{1,0:T(8,128)(2,1)S(1)}, bf16[1024,384]{1,0:T(8,128)(2,1)S(1)}, u32[]{:S(2)}, u32[]{:S(2)}) collective-permute-start(bf16[1024,384]{1,0:T(8,128)(2,1)S(1)} %collective-permute-done), channel_id=1, source_target_pairs={{1,0},{3,2},{5,4},{7,6},{9,8},{11,10},{13,12},{17,16},{19,18},{21,... | collective-permute-start | bytes 2359304 | tf_op jit(solution)/shard_map/ppermute | solution.py:291
  8.8 0.6 fusion.9
  9.4 0.7 exponential_convert_fusion.2
  10.2 0.7 exponential_convert_fusion.3
  10.9 1.4 %convert_reduce_fusion.3 = (f32[1024]{0:T(1024)S(1)}, f32[1024]{0:T(1024)S(1)}, bf16[1024,1024]{1,0:T(8,128)(2,1)S(1)}) fusion(bf16[]{:T(256)} %bitcast.1, bf16[512,1024]{1,0:T(8,128)(2,1)S(1)} %exponential_convert_fusion.2, bf16[512,1024]{1,0:T(8,128)(2,1)S(1)} %exponential_convert_fusion.3), kind=kLoop, calls=%fused_computation.3 | loop fusion | flops 9435136 | bytes 4202498 | tf_op jit(solution)/shard_map/reduce_sum | solution.py:300
  12.3 19.1 %collective-permute-start.3 = (f32[1024]{0:T(1024)S(1)}, f32[1024]{0:T(1024)S(1)}, u32[]{:S(2)}, u32[]{:S(2)}) collective-permute-start(f32[1024]{0:T(1024)S(1)} %get-tuple-element.3), channel_id=1, source_target_pairs={{0,1},{1,2},{2,3},{3,4},{4,5},{5,6},{6,7},{7,8},{8,9},{9,10},{10,1... | collective-permute-start | bytes 12296 | tf_op jit(solution)/shard_map/ppermute | solution.py:260
  31.4 0.0 collective-permute-done.2
  31.4 0.0 collective-permute-done.1
  31.4 0.8 exponential_convert_fusion.1
  32.2 0.8 exponential_convert_fusion
  33.0 2.6 %convert_reduce_fusion.1 = (f32[1024]{0:T(1024)S(1)}, f32[1024]{0:T(1024)S(1)}, bf16[1024,1024]{1,0:T(8,128)(2,1)}) fusion(bf16[]{:T(256)} %bitcast.2, bf16[512,1024]{1,0:T(8,128)(2,1)S(1)} %exponential_convert_fusion, bf16[512,1024]{1,0:T(8,128)(2,1)S(1)} %exponential_convert_fusion.1), kind=kLoop, calls=%fused_computation.1 | loop fusion | flops 9435136 | bytes 4202498 | tf_op jit(solution)/shard_map/reduce_sum | solution.py:300
  35.6 0.0 copy-start
  35.6 4.1 %collective-permute-start.4 = (f32[1024]{0:T(1024)S(1)}, f32[1024]{0:T(1024)S(1)}, u32[]{:S(2)}, u32[]{:S(2)}) collective-permute-start(f32[1024]{0:T(1024)S(1)} %get-tuple-element.5), channel_id=1, source_target_pairs={{0,2},{1,3},{2,4},{3,5},{4,6},{5,7},{6,8},{7,9},{8,10},{9,11},{10,... | collective-permute-start | bytes 12296 | tf_op jit(solution)/shard_map/ppermute | solution.py:260
  39.7 0.3 convert_reduce_fusion.4
  40.1 0.0 collective-permute-done.3
  40.1 1.0 collective-permute-done.4
  41.0 0.6 fusion.8
  41.6 0.0 copy-done
  41.6 61.1 %iterations.1 = f32[64,1024]{1,0:T(8,128)S(1)} custom-call(f32[64,1024]{1,0:T(8,128)S(1)} %bitcast.10, f32[1,1024]{1,0:T(1,128)S(1)} %bitcast.11, bf16[1024,1024]{1,0:T(8,128)(2,1)S(1)} %pad_maximum_fusion.refs_0_, bf16[1024,1024]{1,0:T(8,128)(2,1)S(1)} %get-tuple-element.8.refs_1_, bf16[1024,1024]{1,0:T(8,128)(2,1)} %get-tuple-element.9.refs_2_), custom_call_target="tpu_custom_call" | custom-call | tf_op jit(solution)/shard_map/iterations/pallas_call | solution.py:231
  102.7 0.7 copy.6
  (2 shorter events, 0.0 us)
Async XLA Ops:
  0.6 4.8 %copy-start.1 = (s32[1,2]{1,0:T(1,128)S(1)}, s32[1,2]{1,0:T(1,128)}, u32[]{:S(2)}) copy-start(s32[1,2]{1,0:T(1,128)} %param.5) | copy-start | bytes 28
  3.4 4.2 %collective-permute-start = (bf16[1024,384]{1,0:T(8,128)(2,1)S(1)}, bf16[1024,384]{1,0:T(8,128)(2,1)S(1)}, u32[]{:S(2)}, u32[]{:S(2)}) collective-permute-start(bf16[1024,384]{1,0:T(8,128)(2,1)S(1)} %fusion.1), channel_id=1, source_target_pairs={{1,0},{2,1},{3,2},{4,3},{5,4},{6,5},{7,6},{8,7},{9,8},{10,9},{11,1... | collective-permute-start | bytes 2359304 | tf_op jit(solution)/shard_map/ppermute | solution.py:260
  4.7 26.8 %collective-permute-start.2 = (bf16[1024,384]{1,0:T(8,128)(2,1)S(1)}, bf16[1024,384]{1,0:T(8,128)(2,1)S(1)}, u32[]{:S(2)}, u32[]{:S(2)}) collective-permute-start(bf16[1024,384]{1,0:T(8,128)(2,1)S(1)} %fusion.1), channel_id=1, source_target_pairs={{3,1},{5,3},{7,5},{9,7},{11,9},{13,11},{15,13},{19,17},{21,19},{23... | collective-permute-start | bytes 2359304 | tf_op jit(solution)/shard_map/ppermute | solution.py:290
  7.5 23.9 %collective-permute-start.1 = (bf16[1024,384]{1,0:T(8,128)(2,1)S(1)}, bf16[1024,384]{1,0:T(8,128)(2,1)S(1)}, u32[]{:S(2)}, u32[]{:S(2)}) collective-permute-start(bf16[1024,384]{1,0:T(8,128)(2,1)S(1)} %collective-permute-done), channel_id=1, source_target_pairs={{1,0},{3,2},{5,4},{7,6},{9,8},{11,10},{13,12},{17,16},{19,18},{21,... | collective-permute-start | bytes 2359304 | tf_op jit(solution)/shard_map/ppermute | solution.py:291
  12.3 27.8 %collective-permute-start.3 = (f32[1024]{0:T(1024)S(1)}, f32[1024]{0:T(1024)S(1)}, u32[]{:S(2)}, u32[]{:S(2)}) collective-permute-start(f32[1024]{0:T(1024)S(1)} %get-tuple-element.3), channel_id=1, source_target_pairs={{0,1},{1,2},{2,3},{3,4},{4,5},{5,6},{6,7},{7,8},{8,9},{9,10},{10,1... | collective-permute-start | bytes 12296 | tf_op jit(solution)/shard_map/ppermute | solution.py:260
  35.6 6.0 %copy-start = (f32[1024,64]{0,1:T(8,128)S(1)}, f32[1024,64]{0,1:T(8,128)}, u32[]{:S(2)}) copy-start(f32[1024,64]{0,1:T(8,128)} %param.4) | copy-start | bytes 786436
  35.6 5.4 %collective-permute-start.4 = (f32[1024]{0:T(1024)S(1)}, f32[1024]{0:T(1024)S(1)}, u32[]{:S(2)}, u32[]{:S(2)}) collective-permute-start(f32[1024]{0:T(1024)S(1)} %get-tuple-element.5), channel_id=1, source_target_pairs={{0,2},{1,3},{2,4},{3,5},{4,6},{5,7},{6,8},{7,9},{8,10},{9,11},{10,... | collective-permute-start | bytes 12296 | tf_op jit(solution)/shard_map/ppermute | solution.py:260
